TPU v7x, 128 devices: a whole 4x4x4 slice. The times are simulated.
128 devices in a mesh: pitch: 8 (over y, x_hi), span: 4 (over z), axial: 4 (over x_lo, core).
Axes of the slice: x: 4 (x_hi: 2, x_lo: 2; x = x_hi * 2 + x_lo), y: 4, z: 4, core: 2. Of those that a mesh axis runs over, the one named last changes fastest.
Arguments:
- guess: float32 [2, 6, 64, 64, 512], P(None, None, 'pitch', 'span', 'axial'), may hold values from -6 to 6
- right_side: float32 [2, 6, 64, 64, 512], P(None, None, 'pitch', 'span', 'axial'), may hold values from -60 to 60
- diag_block: bfloat16 [6, 6, 64, 64, 512], P(None, None, 'pitch', 'span', 'axial'), may hold values from -4 to 4
- neighbour_blocks: bfloat16 [6, 6, 6, 64, 64, 512], P(None, None, None, 'pitch', 'span', 'axial'), may hold values from -0.6484375 to 0.6484375
- dissipation: float32 [3, 64, 64, 512], P(None, 'pitch', 'span', 'axial'), may hold values from 0.03 to 0.25
- omega_volume: float32 [64, 64, 512], P('pitch', 'span', 'axial'), may hold values from 0.2 to 2
- pseudo_step: float32 [64, 64, 512], P('pitch', 'span', 'axial'), may hold values from 0.03 to 0.3
- phase: float32 [1], replicated, may hold values from -3.140625 to 3.140625
Outputs:
- solution_field: float32 [2, 6, 64, 64, 512], P(None, None, 'pitch', 'span', 'axial')
- norms: float32 [2], replicated
All inputs are finite; a program needn't handle non-finite values.
Results may differ from a plain program's by a relative error of at most 0.0003.
Values sent between devices are 32-bit elements; how exact they have to be, the bound alone decides.
A program may use at most 128 MiB of HBM per device.

v0:
```python
import jax
import jax.numpy as jnp
from jax import lax
from jax.sharding import PartitionSpec as P

ITERS = 2


def extended_2(cells, sides, width):
    for axis, dim in sides:
        count = lax.axis_size(axis)
        head = lax.slice_in_dim(cells, 0, width, axis=dim)
        tail = lax.slice_in_dim(cells, cells.shape[dim] - width, cells.shape[dim], axis=dim)
        cells = jnp.concatenate(
            [
                lax.ppermute(tail, axis, [(i, (i + 1) % count) for i in range(count)]),
                cells,
                lax.ppermute(head, axis, [((i + 1) % count, i) for i in range(count)]),
            ],
            axis=dim,
        )
    return cells


def block_apply(blocks, vector_in):
    summed = None
    for column in range(blocks.shape[1]):
        product = blocks[:, column].astype(jnp.float32)[None] * vector_in[:, column][:, None]
        summed = product if summed is None else summed + product
    return summed


def rotate(values, cosine, sine_part):
    real_part = values[0]
    imag_part = values[1]
    return jnp.stack(
        [cosine * real_part - sine_part * imag_part, sine_part * real_part + cosine * imag_part]
    )


def operate(
    current, pitch_ext, span_ext, axial_ext, diag_block, neighbour_blocks, dissipation, omega_volume
):
    summed = block_apply(diag_block, current)
    summed = (
        summed
        + block_apply(neighbour_blocks[0], pitch_ext[:, :, 1:-3])
        + block_apply(neighbour_blocks[1], pitch_ext[:, :, 3:-1])
    )
    summed = (
        summed
        + block_apply(neighbour_blocks[2], span_ext[:, :, :, 1:-3])
        + block_apply(neighbour_blocks[3], span_ext[:, :, :, 3:-1])
    )
    summed = (
        summed
        + block_apply(neighbour_blocks[4], axial_ext[:, :, :, :, 1:-3])
        + block_apply(neighbour_blocks[5], axial_ext[:, :, :, :, 3:-1])
    )
    summed = summed + dissipation[0] * (pitch_ext[:, :, :-4] + pitch_ext[:, :, 4:])
    summed = summed + dissipation[1] * (span_ext[:, :, :, :-4] + span_ext[:, :, :, 4:])
    summed = summed + dissipation[2] * (axial_ext[:, :, :, :, :-4] + axial_ext[:, :, :, :, 4:])
    rotation_term = jnp.stack([-omega_volume * current[1], omega_volume * current[0]])
    return summed + rotation_term


def extended(current):
    padded = extended_2(current, (("pitch", 2), ("span", 3), ("axial", 4)), 2)
    pitch_ext = padded[:, :, :, 2:-2, 2:-2]
    span_ext = padded[:, :, 2:-2, :, 2:-2]
    axial_ext = padded[:, :, 2:-2, 2:-2, :]
    first_span = lax.axis_index("span") == 0
    last_span = lax.axis_index("span") == lax.axis_size("span") - 1
    span_ext = jnp.concatenate(
        [
            jnp.where(first_span, 0.0, span_ext[:, :, :, :2]),
            span_ext[:, :, :, 2:-2],
            jnp.where(last_span, 0.0, span_ext[:, :, :, -2:]),
        ],
        axis=3,
    )
    first_axial = lax.axis_index("axial") == 0
    last_axial = lax.axis_index("axial") == lax.axis_size("axial") - 1
    axial_ext = jnp.concatenate(
        [
            jnp.where(first_axial, 0.0, axial_ext[:, :, :, :, :2]),
            axial_ext[:, :, :, :, 2:-2],
            jnp.where(last_axial, 0.0, axial_ext[:, :, :, :, -2:]),
        ],
        axis=4,
    )
    return (pitch_ext, span_ext, axial_ext)


def body(
    guess, right_side, diag_block, neighbour_blocks, dissipation, omega_volume, pseudo_step, phase
):
    cosine = jnp.cos(phase[0])
    sine_part = jnp.sin(phase[0])
    first_pitch = lax.axis_index("pitch") == 0
    last_pitch = lax.axis_index("pitch") == lax.axis_size("pitch") - 1
    current = guess
    global_sums = []
    for iteration in range(ITERS):
        pitch_ext, span_ext, axial_ext = extended(current)
        lower_rim = jnp.where(
            first_pitch, rotate(pitch_ext[:, :, :2], cosine, -sine_part), pitch_ext[:, :, :2]
        )
        upper_rim = jnp.where(
            last_pitch, rotate(pitch_ext[:, :, -2:], cosine, sine_part), pitch_ext[:, :, -2:]
        )
        pitch_ext = jnp.concatenate([lower_rim, pitch_ext[:, :, 2:-2], upper_rim], axis=2)
        residual = right_side - operate(
            current,
            pitch_ext,
            span_ext,
            axial_ext,
            diag_block,
            neighbour_blocks,
            dissipation,
            omega_volume,
        )
        local_square = jnp.sum(residual * residual)
        global_sums.append(lax.psum(local_square, ("pitch", "span", "axial")))
        current = current + pseudo_step[None, None] * residual
    totals = jnp.stack(global_sums)
    cell_count = float(
        guess.size * lax.axis_size("pitch") * lax.axis_size("span") * lax.axis_size("axial")
    )
    norms = jnp.sqrt(totals / cell_count)
    return (current, norms)


def solution(mesh):
    placed = (
        P(None, None, "pitch", "span", "axial"),
        P(None, None, "pitch", "span", "axial"),
        P(None, None, "pitch", "span", "axial"),
        P(None, None, None, "pitch", "span", "axial"),
        P(None, "pitch", "span", "axial"),
        P("pitch", "span", "axial"),
        P("pitch", "span", "axial"),
        P(),
    )
    return jax.shard_map(
        body,
        mesh=mesh,
        in_specs=placed,
        out_specs=(P(None, None, "pitch", "span", "axial"), P()),
        check_vma=False,
    )
```

profile of v0, /device:TPU:1, one launch (start us, length us, event | category | flops | bytes accessed | tf_op | source)
XLA Modules:
  0.0 194.3 jit_solution(15869645522593865707)
XLA Ops:
  0.6 1.9 fusion.63
  2.5 3.6 %collective-permute-start = (f32[2,6,2,16,128]{4,3,2,1,0:T(8,128)}, f32[2,6,2,16,128]{4,3,2,1,0:T(8,128)S(1)}, u32[]{:S(2)}, u32[]{:S(2)}) collective-permute-start(f32[2,6,2,16,128]{4,3,2,1,0:T(8,128)} %get-tuple-element.154), channel_id=1, source_target_pairs={{0,16},{16,32},{32,48},{48,64},{64,80},{80,96},{96,112},{112,0},{1... | collective-permute-start | bytes 589832 | tf_op jit(solution)/shard_map/ppermute | solution.py:16
  6.1 2.5 %collective-permute-start.1 = (f32[2,6,2,16,128]{4,3,2,1,0:T(8,128)}, f32[2,6,2,16,128]{4,3,2,1,0:T(8,128)S(1)}, u32[]{:S(2)}, u32[]{:S(2)}) collective-permute-start(f32[2,6,2,16,128]{4,3,2,1,0:T(8,128)} %get-tuple-element.155), channel_id=1, source_target_pairs={{16,0},{32,16},{48,32},{64,48},{80,64},{96,80},{112,96},{0,112},{1... | collective-permute-start | bytes 589832 | tf_op jit(solution)/shard_map/ppermute | solution.py:18
  11.7 5.1 %slice_bitcast_fusion.5 = (bf16[6,6,8,16,128]{4,3,2,1,0:T(8,128)(2,1)S(1)}, bf16[6,6,8,16,128]{4,3,2,1,0:T(8,128)(2,1)S(1)}, bf16[6,6,8,16,128]{4,3,2,1,0:T(8,12...) fusion(bf16[6,6,6,8,16,128]{5,4,3,2,1,0:T(8,128)(2,1)} %param.11), kind=kLoop, calls=%fused_computation.7 | loop fusion | bytes 14155776 | tf_op jit(solution)/shard_map/squeeze | solution.py:47
  19.5 1.6 fusion.44
  22.5 1.5 fusion.32
  24.0 1.5 fusion.26
  29.5 1.7 collective-permute-start.2
  31.2 2.2 %collective-permute-start.3 = (f32[2,6,12,2,128]{4,2,3,1,0:T(8,128)S(1)}, f32[2,6,12,2,128]{4,2,3,1,0:T(8,128)S(1)}, u32[]{:S(2)}, u32[]{:S(2)}) collective-permute-start(f32[2,6,12,2,128]{4,2,3,1,0:T(8,128)S(1)} %get-tuple-element.95), channel_id=1, source_target_pairs={{4,0},{8,4},{12,8},{0,12},{5,1},{9,5},{13,9},{1,13},{6,2},{10,6},{... | collective-permute-start | bytes 442376 | tf_op jit(solution)/shard_map/ppermute | solution.py:18
  35.4 2.0 %collective-permute-done.2 = f32[2,6,12,2,128]{4,2,3,1,0:T(8,128)S(1)} collective-permute-done((f32[2,6,12,2,128]{4,2,3,1,0:T(8,128)S(1)}, f32[2,6,12,2,128]{4,2,3,1,0:T(8,128)S(1)}, u32[]{:S(2)}, u32[]{:S(2)}) %collective-permute-start.2) | collective-permute-done | bytes 147488 | tf_op jit(solution)/shard_map/ppermute | solution.py:16
  39.1 1.9 fusion.60
  41.1 3.5 %copy.102 = f32[2,6,12,20,2]{3,2,4,1,0:T(8,128)} copy(f32[2,6,12,20,2]{4,2,3,1,0:T(8,128)} %get-tuple-element.17) | data formatting | bytes 46080 | tf_op jit(solution)/shard_map/slice | solution.py:12
  44.6 1.7 collective-permute-start.5
  46.3 1.9 copy.100
  49.9 2.3 %slice_bitcast_fusion.53 = (f32[2,8,16,128]{3,2,1,0:T(8,128)}, f32[2,8,16,128]{3,2,1,0:T(8,128)}, f32[2,8,16,128]{3,2,1,0:T(8,128)}, f32[2,8,16,128]{3,2,1,0:T(8...) fusion(f32[2,6,8,18,128]{4,3,2,1,0:T(8,128)} %copy_dynamic-update-slice_fusion), kind=kLoop, calls=%fused_computation.196 | loop fusion | bytes 1572864 | tf_op jit(solution)/shard_map/mul | solution.py:28
  54.8 1.5 maximum_bitcast_fusion.41
  58.6 12.2 %multiply_reduce_fusion.1 = (f32[]{:T(128)}, f32[2,6,8,16,128]{4,3,2,1,0:T(8,128)S(1)}) fusion(f32[2,6,8,16,128]{4,3,2,1,0:T(8,128)} %param.9, f32[1,6,8,16,128]{4,3,2,1,0:T(8,128)} %get-tuple-element.157, f32[1,6,8,16,128]{4,3,2,1,0:T(8,128)} %get-tuple-element.156, f32[2,6,8,16,2]{4,3,2,1,0:T(8,128)S(1)} %copy.103, f32[2,6,8,16,128]{4,3,2,1,0:T(8,128)S(1)} %copy-done, ...), kind=kLoop, calls=%fused_computation.42 | loop fusion | flops 20054016 | bytes 26664964 | tf_op jit(solution)/shard_map/reduce_sum | solution.py:123
  71.4 4.7 %collective-permute-start.7 = (f32[2,6,2,16,128]{4,3,2,1,0:T(8,128)S(1)}, f32[2,6,2,16,128]{4,3,2,1,0:T(8,128)S(1)}, u32[]{:S(2)}, u32[]{:S(2)}) collective-permute-start(f32[2,6,2,16,128]{4,3,2,1,0:T(8,128)S(1)} %get-tuple-element.145), channel_id=1, source_target_pairs={{16,0},{32,16},{48,32},{64,48},{80,64},{96,80},{112,96},{0,112},{1... | collective-permute-start | bytes 589832 | tf_op jit(solution)/shard_map/ppermute | solution.py:18
  77.1 4.5 %collective-permute-done.6 = f32[2,6,2,16,128]{4,3,2,1,0:T(8,128)S(1)} collective-permute-done((f32[2,6,2,16,128]{4,3,2,1,0:T(8,128)S(1)}, f32[2,6,2,16,128]{4,3,2,1,0:T(8,128)S(1)}, u32[]{:S(2)}, u32[]{:S(2)}) %collective-permute-start.6) | collective-permute-done | bytes 196640 | tf_op jit(solution)/shard_map/ppermute | solution.py:16
  81.6 1.7 collective-permute-done.7
  84.9 2.4 %collective-permute-start.9 = (f32[2,6,12,2,128]{4,2,3,1,0:T(8,128)S(1)}, f32[2,6,12,2,128]{4,2,3,1,0:T(8,128)S(1)}, u32[]{:S(2)}, u32[]{:S(2)}) collective-permute-start(f32[2,6,12,2,128]{4,2,3,1,0:T(8,128)S(1)} %copy.106), channel_id=1, source_target_pairs={{4,0},{8,4},{12,8},{0,12},{5,1},{9,5},{13,9},{1,13},{6,2},{10,6},{... | collective-permute-start | bytes 442376 | tf_op jit(solution)/shard_map/ppermute | solution.py:18
  88.3 3.5 %collective-permute-done.8 = f32[2,6,12,2,128]{4,2,3,1,0:T(8,128)S(1)} collective-permute-done((f32[2,6,12,2,128]{4,2,3,1,0:T(8,128)S(1)}, f32[2,6,12,2,128]{4,2,3,1,0:T(8,128)S(1)}, u32[]{:S(2)}, u32[]{:S(2)}) %collective-permute-start.8) | collective-permute-done | bytes 147488 | tf_op jit(solution)/shard_map/ppermute | solution.py:16
  93.4 2.4 %fusion.61 = (f32[2,6,12,20,2]{4,3,2,1,0:T(8,128)}, f32[2,6,12,20,2]{4,3,2,1,0:T(8,128)}) fusion(f32[2,6,12,20,128]{4,3,2,1,0:T(8,128)S(1)} %pad_maximum_fusion.1), kind=kLoop, calls=%fused_computation.245 | loop fusion | bytes 92160 | tf_op jit(solution)/shard_map/slice | solution.py:13
  95.8 2.7 %copy.110 = f32[2,6,12,20,2]{3,2,4,1,0:T(8,128)S(1)} copy(f32[2,6,12,20,2]{4,3,2,1,0:T(8,128)} %get-tuple-element.18) | data formatting | bytes 46080 | tf_op jit(solution)/shard_map/slice | solution.py:13
  100.3 3.4 %copy.112 = f32[2,6,12,20,2]{3,2,4,1,0:T(8,128)} copy(f32[2,6,12,20,2]{4,3,2,1,0:T(8,128)} %get-tuple-element.19) | data formatting | bytes 46080 | tf_op jit(solution)/shard_map/slice | solution.py:12
  104.8 1.5 copy.111
  106.4 1.6 maximum_bitcast_fusion.11
  109.1 1.7 slice_select_fusion
  110.7 1.5 copy.113
  113.8 12.2 %multiply_reduce_fusion = (f32[]{:T(128)}, f32[2,6,8,16,128]{4,3,2,1,0:T(8,128)S(1)}) fusion(f32[2,6,8,16,128]{4,3,2,1,0:T(8,128)} %param.9, f32[1,6,8,16,128]{4,3,2,1,0:T(8,128)} %get-tuple-element.147, f32[1,6,8,16,128]{4,3,2,1,0:T(8,128)} %get-tuple-element.146, f32[2,6,8,16,2]{4,3,2,1,0:T(8,128)S(1)} %copy.113, ...), kind=kLoop, calls=%fused_computation.41 | loop fusion | flops 20250624 | bytes 25976836 | tf_op jit(solution)/shard_map/reduce_sum | solution.py:123
  127.1 65.3 %all-reduce = (f32[1]{0:T(128)}, f32[1]{0:T(128)}) all-reduce(f32[1]{0:T(128)} %bitcast.138, f32[1]{0:T(128)} %bitcast.137), channel_id=1, replica_groups=mesh['pitch'=8,'span'=4,'axial'=4] {'pitch','span','axial'}, use_global_device_ids=true, to_apply=%region_3.4 | all-reduce | flops 2 | bytes 16 | tf_op jit(solution)/shard_map/psum | solution.py:124
  192.4 1.9 fusion.57
  (145 shorter events, 32.9 us)
Async XLA Ops:
  0.6 10.1 %copy-start = (f32[2,6,8,16,128]{4,3,2,1,0:T(8,128)S(1)}, f32[2,6,8,16,128]{4,3,2,1,0:T(8,128)}, u32[]{:S(2)}) copy-start(f32[2,6,8,16,128]{4,3,2,1,0:T(8,128)} %param.8) | copy-start | bytes 2359300
  2.5 26.6 %collective-permute-start = (f32[2,6,2,16,128]{4,3,2,1,0:T(8,128)}, f32[2,6,2,16,128]{4,3,2,1,0:T(8,128)S(1)}, u32[]{:S(2)}, u32[]{:S(2)}) collective-permute-start(f32[2,6,2,16,128]{4,3,2,1,0:T(8,128)} %get-tuple-element.154), channel_id=1, source_target_pairs={{0,16},{16,32},{32,48},{48,64},{64,80},{80,96},{96,112},{112,0},{1... | collective-permute-start | bytes 589832 | tf_op jit(solution)/shard_map/ppermute | solution.py:16
  6.1 23.2 %collective-permute-start.1 = (f32[2,6,2,16,128]{4,3,2,1,0:T(8,128)}, f32[2,6,2,16,128]{4,3,2,1,0:T(8,128)S(1)}, u32[]{:S(2)}, u32[]{:S(2)}) collective-permute-start(f32[2,6,2,16,128]{4,3,2,1,0:T(8,128)} %get-tuple-element.155), channel_id=1, source_target_pairs={{16,0},{32,16},{48,32},{64,48},{80,64},{96,80},{112,96},{0,112},{1... | collective-permute-start | bytes 589832 | tf_op jit(solution)/shard_map/ppermute | solution.py:18
  24.0 2.0 %copy-start.11 = (bf16[6,6,8,16,128]{4,3,2,1,0:T(8,128)(2,1)S(1)}, bf16[6,6,8,16,128]{4,3,2,1,0:T(8,128)(2,1)}, u32[]{:S(2)}) copy-start(bf16[6,6,8,16,128]{4,3,2,1,0:T(8,128)(2,1)} %param.10) | copy-start | bytes 3538948
  26.0 1.4 copy-start.17
  27.5 2.0 %copy-start.19 = (f32[8,16,128]{2,1,0:T(8,128)}, f32[8,16,128]{2,1,0:T(8,128)S(1)}, u32[]{:S(2)}) copy-start(f32[8,16,128]{2,1,0:T(8,128)S(1)} %neg.9) | copy-start | bytes 196612
  29.5 8.0 %collective-permute-start.2 = (f32[2,6,12,2,128]{4,2,3,1,0:T(8,128)S(1)}, f32[2,6,12,2,128]{4,2,3,1,0:T(8,128)S(1)}, u32[]{:S(2)}, u32[]{:S(2)}) collective-permute-start(f32[2,6,12,2,128]{4,2,3,1,0:T(8,128)S(1)} %get-tuple-element.94), channel_id=1, source_target_pairs={{0,4},{4,8},{8,12},{12,0},{1,5},{5,9},{9,13},{13,1},{2,6},{6,10},{... | collective-permute-start | bytes 442376 | tf_op jit(solution)/shard_map/ppermute | solution.py:16
  31.2 6.3 %collective-permute-start.3 = (f32[2,6,12,2,128]{4,2,3,1,0:T(8,128)S(1)}, f32[2,6,12,2,128]{4,2,3,1,0:T(8,128)S(1)}, u32[]{:S(2)}, u32[]{:S(2)}) collective-permute-start(f32[2,6,12,2,128]{4,2,3,1,0:T(8,128)S(1)} %get-tuple-element.95), channel_id=1, source_target_pairs={{4,0},{8,4},{12,8},{0,12},{5,1},{9,5},{13,9},{1,13},{6,2},{10,6},{... | collective-permute-start | bytes 442376 | tf_op jit(solution)/shard_map/ppermute | solution.py:18
  33.5 2.0 %copy-start.9 = (f32[2,6,2,16,128]{4,3,2,1,0:T(8,128)}, f32[2,6,2,16,128]{4,3,2,1,0:T(8,128)S(1)}, u32[]{:S(2)}) copy-start(f32[2,6,2,16,128]{4,3,2,1,0:T(8,128)S(1)} %maximum_select_fusion) | copy-start | bytes 589828
  33.5 1.9 copy-start.10
  41.1 8.1 %copy-start.36 = (f32[2,6,12,2,128]{4,2,3,1,0:T(8,128)S(1)}, f32[2,6,12,2,128]{4,2,3,1,0:T(8,128)}, u32[]{:S(2)}) copy-start(f32[2,6,12,2,128]{4,2,3,1,0:T(8,128)} %copy-done.35) | copy-start | bytes 442372
  44.6 8.6 %collective-permute-start.5 = (f32[2,6,12,20,2]{3,2,4,1,0:T(8,128)}, f32[2,6,12,20,2]{3,2,4,1,0:T(8,128)}, u32[]{:S(2)}, u32[]{:S(2)}) collective-permute-start(f32[2,6,12,20,2]{3,2,4,1,0:T(8,128)} %copy.102), channel_id=1, source_target_pairs={{1,0},{2,1},{3,2},{0,3},{5,4},{6,5},{7,6},{4,7},{9,8},{10,9},{11,1... | collective-permute-start | bytes 69128 | tf_op jit(solution)/shard_map/ppermute | solution.py:18
  46.3 5.9 %copy-start.34 = (f32[2,6,12,2,128]{4,2,3,1,0:T(8,128)S(1)}, f32[2,6,12,2,128]{4,2,3,1,0:T(8,128)}, u32[]{:S(2)}) copy-start(f32[2,6,12,2,128]{4,2,3,1,0:T(8,128)} %copy-done.33) | copy-start | bytes 442372
  48.2 8.2 %collective-permute-start.4 = (f32[2,6,12,20,2]{3,2,4,1,0:T(8,128)}, f32[2,6,12,20,2]{3,2,4,1,0:T(8,128)S(1)}, u32[]{:S(2)}, u32[]{:S(2)}) collective-permute-start(f32[2,6,12,20,2]{3,2,4,1,0:T(8,128)} %copy.100), channel_id=1, source_target_pairs={{0,1},{1,2},{2,3},{3,0},{4,5},{5,6},{6,7},{7,4},{8,9},{9,10},{10,1... | collective-permute-start | bytes 69128 | tf_op jit(solution)/shard_map/ppermute | solution.py:16
  52.2 4.1 %copy-start.14 = (f32[2,6,8,2,128]{4,3,2,1,0:T(2,128)}, f32[2,6,8,2,128]{4,3,2,1,0:T(2,128)S(1)}, u32[]{:S(2)}) copy-start(f32[2,6,8,2,128]{4,3,2,1,0:T(2,128)S(1)} %copy.98) | copy-start | bytes 294916
  58.6 12.2 %copy-start.37 = (f32[8,16,128]{2,1,0:T(8,128)S(1)}, f32[8,16,128]{2,1,0:T(8,128)}, u32[]{:S(2)}) copy-start(f32[8,16,128]{2,1,0:T(8,128)} %param.14) | copy-start | bytes 196612
  70.8 5.3 %copy-start.18 = (f32[8,16,128]{2,1,0:T(8,128)S(1)}, f32[8,16,128]{2,1,0:T(8,128)}, u32[]{:S(2)}) copy-start(f32[8,16,128]{2,1,0:T(8,128)} %param.13) | copy-start | bytes 196612
  70.8 5.3 %copy-start.20 = (f32[8,16,128]{2,1,0:T(8,128)S(1)}, f32[8,16,128]{2,1,0:T(8,128)}, u32[]{:S(2)}) copy-start(f32[8,16,128]{2,1,0:T(8,128)} %copy-done.19) | copy-start | bytes 196612
  71.0 10.6 %collective-permute-start.6 = (f32[2,6,2,16,128]{4,3,2,1,0:T(8,128)S(1)}, f32[2,6,2,16,128]{4,3,2,1,0:T(8,128)S(1)}, u32[]{:S(2)}, u32[]{:S(2)}) collective-permute-start(f32[2,6,2,16,128]{4,3,2,1,0:T(8,128)S(1)} %get-tuple-element.144), channel_id=1, source_target_pairs={{0,16},{16,32},{32,48},{48,64},{64,80},{80,96},{96,112},{112,0},{1... | collective-permute-start | bytes 589832 | tf_op jit(solution)/shard_map/ppermute | solution.py:16
  71.4 11.8 %collective-permute-start.7 = (f32[2,6,2,16,128]{4,3,2,1,0:T(8,128)S(1)}, f32[2,6,2,16,128]{4,3,2,1,0:T(8,128)S(1)}, u32[]{:S(2)}, u32[]{:S(2)}) collective-permute-start(f32[2,6,2,16,128]{4,3,2,1,0:T(8,128)S(1)} %get-tuple-element.145), channel_id=1, source_target_pairs={{16,0},{32,16},{48,32},{64,48},{80,64},{96,80},{112,96},{0,112},{1... | collective-permute-start | bytes 589832 | tf_op jit(solution)/shard_map/ppermute | solution.py:18
  84.4 7.3 %collective-permute-start.8 = (f32[2,6,12,2,128]{4,2,3,1,0:T(8,128)S(1)}, f32[2,6,12,2,128]{4,2,3,1,0:T(8,128)S(1)}, u32[]{:S(2)}, u32[]{:S(2)}) collective-permute-start(f32[2,6,12,2,128]{4,2,3,1,0:T(8,128)S(1)} %copy.104), channel_id=1, source_target_pairs={{0,4},{4,8},{8,12},{12,0},{1,5},{5,9},{9,13},{13,1},{2,6},{6,10},{... | collective-permute-start | bytes 442376 | tf_op jit(solution)/shard_map/ppermute | solution.py:16
  84.9 8.0 %collective-permute-start.9 = (f32[2,6,12,2,128]{4,2,3,1,0:T(8,128)S(1)}, f32[2,6,12,2,128]{4,2,3,1,0:T(8,128)S(1)}, u32[]{:S(2)}, u32[]{:S(2)}) collective-permute-start(f32[2,6,12,2,128]{4,2,3,1,0:T(8,128)S(1)} %copy.106), channel_id=1, source_target_pairs={{4,0},{8,4},{12,8},{0,12},{5,1},{9,5},{13,9},{1,13},{6,2},{10,6},{... | collective-permute-start | bytes 442376 | tf_op jit(solution)/shard_map/ppermute | solution.py:18
  87.3 5.5 %copy-start.8 = (f32[2,6,2,16,128]{4,3,2,1,0:T(8,128)}, f32[2,6,2,16,128]{4,3,2,1,0:T(8,128)S(1)}, u32[]{:S(2)}) copy-start(f32[2,6,2,16,128]{4,3,2,1,0:T(8,128)S(1)} %maximum_select_fusion.3) | copy-start | bytes 589828
  91.9 1.5 copy-start.12
  92.9 6.4 %copy-start.13 = (f32[2,6,8,2,128]{4,3,2,1,0:T(2,128)}, f32[2,6,8,2,128]{4,3,2,1,0:T(2,128)S(1)}, u32[]{:S(2)}) copy-start(f32[2,6,8,2,128]{4,3,2,1,0:T(2,128)S(1)} %copy.107) | copy-start | bytes 294916
  98.5 5.6 %collective-permute-start.10 = (f32[2,6,12,20,2]{3,2,4,1,0:T(8,128)S(1)}, f32[2,6,12,20,2]{3,2,4,1,0:T(8,128)S(1)}, u32[]{:S(2)}, u32[]{:S(2)}) collective-permute-start(f32[2,6,12,20,2]{3,2,4,1,0:T(8,128)S(1)} %copy.110), channel_id=1, source_target_pairs={{0,1},{1,2},{2,3},{3,0},{4,5},{5,6},{6,7},{7,4},{8,9},{9,10},{10,1... | collective-permute-start | bytes 69128 | tf_op jit(solution)/shard_map/ppermute | solution.py:16
  103.6 5.4 %collective-permute-start.11 = (f32[2,6,12,20,2]{3,2,4,1,0:T(8,128)}, f32[2,6,12,20,2]{3,2,4,1,0:T(8,128)}, u32[]{:S(2)}, u32[]{:S(2)}) collective-permute-start(f32[2,6,12,20,2]{3,2,4,1,0:T(8,128)} %copy.112), channel_id=1, source_target_pairs={{1,0},{2,1},{3,2},{0,3},{5,4},{6,5},{7,6},{4,7},{9,8},{10,9},{11,1... | collective-permute-start | bytes 69128 | tf_op jit(solution)/shard_map/ppermute | solution.py:18
  106.4 1.6 copy-start.1
  112.2 1.4 copy-start.5
  112.3 1.6 copy-start.6
  112.3 1.6 copy-start.16
  113.8 12.2 %copy-start.38 = (f32[8,16,128]{2,1,0:T(8,128)S(1)}, f32[8,16,128]{2,1,0:T(8,128)}, u32[]{:S(2)}) copy-start(f32[8,16,128]{2,1,0:T(8,128)} %param.14) | copy-start | bytes 196612
  (20 other events, 22.5 us)
where the time goes:
time: 195 us; the launch traced here: 194 us
  blocking collectives  65.3 us (33%)
  other arithmetic  54.7 us (28%)
  local copies, waits for them, and re-layouts  37.7 us (19%)
  starting transfers between devices  21.9 us (11%)
  waiting for transfers between devices  12.8 us (7%)
    psum x1, blocking collectives, body(): global_sums.append(lax.psum(local_square, ('pitch', 'span', 'axial')))  65.3 us
    reduce_sum x2, other arithmetic, body(): local_square = jnp.sum(residual * residual)  24.4 us
    ppermute x6, starting transfers between devices, extended_2(): lax.ppermute(head, axis, [((i + 1) % count, i) for i in range(count)])  14 us
    slice x7, local copies, waits for them, and re-layouts, extended_2(): lax.slice_in_dim(cells, cells.shape[dim] - width, cells.shape[dim], axis=...  10.9 us
    mul x11, other arithmetic, block_apply(): blocks[:, column].astype(jnp.float32)[None] * vector_in[:, column][:, None]  10.7 us
    convert_element_type x7, other arithmetic, block_apply(): blocks[:, column].astype(jnp.float32)[None] * vector_in[:, column][:, None]  10.1 us
    ppermute x6, waiting for transfers between devices, extended_2(): lax.ppermute(tail, axis, [(i, (i + 1) % count) for i in range(count)])  9.99 us
    ppermute x6, starting transfers between devices, extended_2(): lax.ppermute(tail, axis, [(i, (i + 1) % count) for i in range(count)])  7.91 us
  transfers between devices with their start and end apart: 12, of which 5 were waited for; matrix products, arithmetic and copies ran while one was open for 21% of the time, Pallas kernels for 0%

commit v1 on v0

v1 whole, which is shorter than its diff:
```python
import functools

import jax
import jax.numpy as jnp
from jax import lax
from jax.experimental import pallas as pl
from jax.experimental.pallas import tpu as pltpu
from jax.sharding import PartitionSpec as P

ITERS = 2
MESH = pl.DeviceIdType.MESH
F32 = jnp.float32


def kernel(
    guess, right_h, diag_h, neigh_h, diss_h, omega_h, pseudo_h, phase,
    out, norms,
    st, hal, prt, rs, dg, nb, ds, om, ps, axs, axr, sq, red, tot_s,
    ld_sem, psend, precv, zsend, zrecv, asend, arecv, rsend, rrecv, ready,
):
    p, s, a = lax.axis_index("pitch"), lax.axis_index("span"), lax.axis_index("axial")
    size_p, size_s, size_a = lax.axis_size("pitch"), lax.axis_size("span"), lax.axis_size("axial")
    y, x_hi = p // 2, lax.rem(p, 2)
    lower, upper = lax.rem(p + size_p - 1, size_p), lax.rem(p + 1, size_p)

    def row_peer(d):
        k = lax.rem(x_hi * size_a + a + d, 2 * size_a)
        return (y * 2 + k // size_a, s, lax.rem(k, size_a))

    def plane_peer(d):
        dy, dz = d // 4, d % 4
        return (lax.rem(p + 2 * dy, size_p), lax.rem(s + dz, size_s), a)

    other = lax.rem(p - 1 + 2 * x_hi + size_p, size_p)
    bar = pltpu.get_barrier_semaphore()
    peers = [(other, s, a)]
    peers += [row_peer(d) for d in range(1, 8)]
    peers += [plane_peer(4 * d) for d in range(1, 4)]
    peers += [plane_peer(d) for d in range(1, 4)]
    for peer in peers:
        pl.semaphore_signal(bar, inc=1, device_id=peer, device_id_type=MESH)

    loads = [
        pltpu.make_async_copy(guess, st.at[0, :, :, :, pl.ds(8, 16), :], ld_sem.at[0]),
        pltpu.make_async_copy(diss_h, ds, ld_sem.at[1]),
        pltpu.make_async_copy(omega_h, om, ld_sem.at[2]),
        pltpu.make_async_copy(pseudo_h, ps, ld_sem.at[3]),
        pltpu.make_async_copy(right_h, rs, ld_sem.at[4]),
        pltpu.make_async_copy(diag_h, dg, ld_sem.at[5]),
    ] + [pltpu.make_async_copy(neigh_h.at[d], nb.at[d], ld_sem.at[6 + d]) for d in range(6)]
    for load in loads:
        load.start()

    rows_zero = jnp.zeros((2, 2, 6, 8, 2, 128), F32)
    ax_zero = jnp.zeros((2, 8, 8, 128), F32)

    @pl.when(s == 0)
    def _():
        st[:, :, :, :, 6:8, :] = rows_zero

    @pl.when(s == size_s - 1)
    def _():
        st[:, :, :, :, 24:26, :] = rows_zero

    @pl.when(a == 0)
    def _():
        axr[:, 0] = ax_zero

    @pl.when(a == size_a - 1)
    def _():
        axr[:, 1] = ax_zero

    sq[...] = jnp.zeros((2, 8, 128), F32)
    angle = jnp.full((8, 128), phase[0], F32)
    cosine, sine = jnp.cos(angle), jnp.sin(angle)
    first, last = p == 0, p == size_p - 1
    turn = (
        (jnp.where(first, cosine, 1.0), jnp.where(first, -sine, 0.0)),
        (jnp.where(last, cosine, 1.0), jnp.where(last, sine, 0.0)),
    )
    lane = lax.broadcasted_iota(jnp.int32, (8, 128), 1)
    lane16 = lax.broadcasted_iota(jnp.int32, (16, 128), 1)

    pl.semaphore_wait(bar, len(peers))

    def pitch_copy(it, way, t):
        layers = pl.ds(0, 2) if way == 0 else pl.ds(6, 2)
        if it == 0:
            src = guess.at[:, :, layers, pl.ds(8 * t, 8), :]
        else:
            src = st.at[1, :, :, layers, pl.ds(8 + 8 * t, 8), :]
        return pltpu.make_async_remote_copy(
            src_ref=src,
            dst_ref=hal.at[it, 1 - way, :, :, :, pl.ds(8 * t, 8), :],
            send_sem=psend.at[it, way, t],
            recv_sem=precv.at[it, 1 - way, t],
            device_id=(lower if way == 0 else upper, s, a),
            device_id_type=MESH,
        )

    groups = ((2, 4), (0, 2), (6, 2))

    def span_copy(it, way, group):
        first_layer, count = (0, 8) if it == 0 else groups[group]
        layers = pl.ds(first_layer, count)
        row = 0 if way == 0 else 14
        if it == 0:
            src = guess.at[:, :, layers, pl.ds(row, 2), :]
        else:
            src = st.at[1, :, :, layers, pl.ds(8 + row, 2), :]
        return pltpu.make_async_remote_copy(
            src_ref=src,
            dst_ref=st.at[it, :, :, layers, pl.ds(24 if way == 0 else 6, 2), :],
            send_sem=zsend.at[it, way, group],
            recv_sem=zrecv.at[it, 1 - way, group],
            device_id=(p, lax.rem(s + (size_s - 1 if way == 0 else 1), size_s), a),
            device_id_type=MESH,
        )

    def axial_copy(it, way, group):
        first_layer, count = (0, 8) if it == 0 else groups[group]
        return pltpu.make_async_remote_copy(
            src_ref=axs.at[it, pl.ds(first_layer, count)],
            dst_ref=axr.at[it, 1 - way, pl.ds(first_layer, count)],
            send_sem=asend.at[it, way, group],
            recv_sem=arecv.at[it, 1 - way, group],
            device_id=(p, s, lax.rem(a + (size_a - 1 if way == 0 else 1), size_a)),
            device_id_type=MESH,
        )

    has_span = (s > 0, s < size_s - 1)
    has_axial = (a > 0, a < size_a - 1)

    def span_start(it, way, group):
        @pl.when(has_span[way])
        def _():
            span_copy(it, way, group).start()

    def axial_start(it, group):
        for way in range(2):
            @pl.when(has_axial[way])
            def _():
                axial_copy(it, way, group).start()

    def side_wait(it, group):
        for way in range(2):
            @pl.when(has_span[way])
            def _():
                span_copy(it, 1 - way, group).wait_recv()

            @pl.when(has_axial[way])
            def _():
                axial_copy(it, 1 - way, group).wait_recv()

    def side_drain(it, group):
        for way in range(2):
            @pl.when(has_span[way])
            def _():
                span_copy(it, way, group).wait_send()

            @pl.when(has_axial[way])
            def _():
                axial_copy(it, way, group).wait_send()

    def pack(it, q):
        packed = jnp.zeros((8, 128), F32)
        for c in range(2):
            for v in range(6):
                for t in range(2):
                    k = (c * 6 + v) * 2 + t
                    tile = st[it, c, v, q, 8 + 8 * t : 16 + 8 * t, :]
                    packed = jnp.where(lane // 4 == k, pltpu.roll(tile, 4 * k + 2, 1), packed)
        axs[it, q] = packed

    def store(it, q, rows, c, residual, state):
        new = state + ps[q, rows, :][None] * residual
        if it == ITERS - 1:
            out[c, :, q, rows, :] = new
        else:
            st[1, c, :, q, pl.ds(8 + rows.start, rows.size), :] = new

    def add_square(it, residuals):
        total = sq[it]
        for residual in residuals:
            total = total + jnp.sum((residual * residual).reshape(-1, 8, 128), axis=0)
        sq[it] = total

    def partial(it, q, low, high, keep):
        acc = [None, None]

        def add(c, term):
            acc[c] = term if acc[c] is None else acc[c] + term

        centre = [st[it, c, :, q, 8:24, :] for c in range(2)]
        mixed = jnp.where(lax.rem(lane, 4) < 2, axr[it, 0, q], axr[it, 1, q])
        far = [[], []]
        for j in range(6):
            blocks = [dg[:, j, q], nb[2, :, j, q], nb[3, :, j, q], nb[4, :, j, q], nb[5, :, j, q]]
            if low >= 1:
                blocks.append(nb[0, :, j, q])
            if high >= 1:
                blocks.append(nb[1, :, j, q])
            blocks = [block.astype(F32) for block in blocks]
            for c in range(2):
                u = st[it, c, j, q, 8:24, :]
                k = (c * 6 + j) * 2
                rim = jnp.concatenate(
                    [pltpu.roll(mixed, (128 - 4 * (k + t) - 2) % 128, 1) for t in range(2)], axis=0
                )
                values = [
                    u,
                    st[it, c, j, q, 7:23, :],
                    st[it, c, j, q, 9:25, :],
                    pltpu.roll(jnp.where(lane16 == 127, rim, u), 1, 1),
                    pltpu.roll(jnp.where(lane16 == 0, rim, u), 127, 1),
                ]
                if low >= 1:
                    values.append(st[it, c, j, q - 1, 8:24, :])
                if high >= 1:
                    values.append(st[it, c, j, q + 1, 8:24, :])
                for block, value in zip(blocks, values):
                    add(c, block * value[None])
                far[c].append(
                    pltpu.roll(jnp.where(lane16 >= 126, rim, u), 2, 1)
                    + pltpu.roll(jnp.where(lane16 < 2, rim, u), 126, 1)
                )
        for c in range(2):
            if low == 2 and high == 2:
                add(c, ds[0, q][None] * (st[it, c, :, q - 2, 8:24, :] + st[it, c, :, q + 2, 8:24, :]))
            elif low == 2:
                add(c, ds[0, q][None] * st[it, c, :, q - 2, 8:24, :])
            else:
                add(c, ds[0, q][None] * st[it, c, :, q + 2, 8:24, :])
            add(c, ds[1, q][None] * (st[it, c, :, q, 6:22, :] + st[it, c, :, q, 10:26, :]))
            add(c, ds[2, q][None] * jnp.stack(far[c]))
        add(0, -(om[q][None] * centre[1]))
        add(1, om[q][None] * centre[0])
        residuals = [rs[c, :, q] - acc[c] for c in range(2)]
        if keep is not None:
            for c in range(2):
                prt[c, :, keep] = residuals[c]
        else:
            for c in range(2):
                store(it, q, pl.ds(0, 16), c, residuals[c], centre[c])
            add_square(it, residuals)

    def faces(it):
        partial(it, 0, 0, 2, 0)
        partial(it, 1, 1, 2, 1)
        partial(it, 6, 2, 1, 2)
        partial(it, 7, 2, 0, 3)

    def inner(it):
        def step(i, carry):
            partial(it, i + 2, 2, 2, None)
            return carry

        lax.fori_loop(0, 4, step, 0)

    def finish(it, face, t):
        rows = pl.ds(8 * t, 8)
        cos_v, sin_v = turn[face]
        near_at, far_at = (1, 0) if face == 0 else (0, 1)

        def rotated(at):
            real, imag = hal[it, face, 0, :, at, rows, :], hal[it, face, 1, :, at, rows, :]
            return [cos_v[None] * real - sin_v[None] * imag, sin_v[None] * real + cos_v[None] * imag]

        near, far = rotated(near_at), rotated(far_at)
        edge, second = (0, 1) if face == 0 else (7, 6)
        keep_edge, keep_second = (0, 1) if face == 0 else (3, 2)
        acc = [ds[0, edge, rows, :][None] * far[c] for c in range(2)]
        for j in range(6):
            block = nb[face, :, j, edge, rows, :].astype(F32)
            for c in range(2):
                acc[c] = acc[c] + block * near[c][j][None]
        squares = []
        for c in range(2):
            residual = prt[c, :, keep_edge, rows, :] - acc[c]
            squares.append(residual)
            store(it, edge, rows, c, residual, st[it, c, :, edge, 8 + 8 * t : 16 + 8 * t, :])
            residual = prt[c, :, keep_second, rows, :] - ds[0, second, rows, :][None] * near[c]
            squares.append(residual)
            store(it, second, rows, c, residual, st[it, c, :, second, 8 + 8 * t : 16 + 8 * t, :])
        add_square(it, squares)

    for t in range(2):
        for way in range(2):
            pitch_copy(0, way, t).start()
    for way in range(2):
        span_start(0, way, 0)
    for d in range(1, 4):
        pl.semaphore_signal(ready, inc=1, device_id=plane_peer(d), device_id_type=MESH)
    loads[0].wait()

    def pack_step(it, base):
        def step(i, carry):
            pack(it, i + base)
            return carry

        return step

    lax.fori_loop(0, 8, pack_step(0, 0), 0)
    axial_start(0, 0)
    for load in loads[1:]:
        load.wait()
    side_wait(0, 0)
    faces(0)
    inner(0)
    for way in range(2):
        span_start(1, way, 0)
    lax.fori_loop(0, 4, pack_step(1, 2), 0)
    axial_start(1, 0)
    for t in range(2):
        for face in range(2):
            pitch_copy(0, 1 - face, t).wait_recv()
            finish(0, face, t)
            pitch_copy(1, face, t).start()
            span_start(1, t, 1 + face)
    lax.fori_loop(0, 2, pack_step(1, 0), 0)
    axial_start(1, 1)
    lax.fori_loop(0, 2, pack_step(1, 6), 0)
    axial_start(1, 2)

    side_wait(1, 0)
    inner(1)
    side_wait(1, 1)
    side_wait(1, 2)
    faces(1)
    for t in range(2):
        for face in range(2):
            pitch_copy(1, 1 - face, t).wait_recv()
            finish(1, face, t)

    half = lax.broadcasted_iota(jnp.int32, (1, 128), 1) < 64

    def folded(it):
        row = jnp.sum(sq[it], axis=0, keepdims=True)
        return row + pltpu.roll(row, 64, 1)

    total = jnp.where(half, folded(0), folded(1))
    row_index, plane_index = x_hi * size_a + a, y * size_s + s
    for stage in range(2):
        count = (8, 16)[stage]
        base = (0, 8)[stage]
        mine = base + (row_index, plane_index)[stage]
        peer_of = (row_peer, plane_peer)[stage]
        tot_s[pl.ds(8 * stage, 1)] = total
        if stage == 1:
            pl.semaphore_wait(ready, 3)
        for d in range(1, count):
            pltpu.make_async_remote_copy(
                src_ref=tot_s.at[pl.ds(8 * stage, 1)],
                dst_ref=red.at[pl.ds(mine, 1)],
                send_sem=rsend.at[stage],
                recv_sem=rrecv.at[stage],
                device_id=peer_of(d),
                device_id_type=MESH,
            ).start()
        got = red.at[pl.ds(base, count - 1)]
        pltpu.make_async_copy(got, got, rrecv.at[stage]).wait()
        rows = red[base : base + count]
        index = lax.broadcasted_iota(jnp.int32, (count, 128), 0) + base
        total = total + jnp.sum(jnp.where(index == mine, 0.0, rows), axis=0, keepdims=True)
    first_sum = jnp.sum(jnp.where(half, total, 0.0), axis=1, keepdims=True)
    second_sum = jnp.sum(jnp.where(half, 0.0, total), axis=1, keepdims=True)
    cells = float(12 * 8 * 16 * 128) * (size_p * size_s * size_a)
    lane1 = lax.broadcasted_iota(jnp.int32, (1, 128), 1)
    norms[...] = jnp.sqrt(jnp.where(lane1 == 0, first_sum, second_sum) / cells)

    for it in range(2):
        for t in range(2):
            for way in range(2):
                pitch_copy(it, way, t).wait_send()
        for group in range(1 if it == 0 else 3):
            side_drain(it, group)
    for stage in range(2):
        count = (8, 16)[stage]
        sent = red.at[pl.ds((0, 8)[stage], count - 1)]
        pltpu.make_async_copy(sent, sent, rsend.at[stage]).wait()


def body(guess, right_side, diag_block, neighbour_blocks, dissipation, omega_volume, pseudo_step, phase):
    anywhere = pl.BlockSpec(memory_space=pl.ANY)
    dma = pltpu.SemaphoreType.DMA
    field, norms = pl.pallas_call(
        kernel,
        out_shape=(
            jax.ShapeDtypeStruct(guess.shape, F32),
            jax.ShapeDtypeStruct((1, 128), F32),
        ),
        in_specs=[anywhere] * 7 + [pl.BlockSpec(memory_space=pltpu.SMEM)],
        out_specs=(
            pl.BlockSpec(memory_space=pltpu.VMEM),
            pl.BlockSpec(memory_space=pltpu.VMEM),
        ),
        scratch_shapes=[
            pltpu.VMEM((2, 2, 6, 8, 32, 128), F32),
            pltpu.VMEM((2, 2, 2, 6, 2, 16, 128), F32),
            pltpu.VMEM((2, 6, 4, 16, 128), F32),
            pltpu.VMEM((2, 6, 8, 16, 128), F32),
            pltpu.VMEM((6, 6, 8, 16, 128), jnp.bfloat16),
            pltpu.VMEM((6, 6, 6, 8, 16, 128), jnp.bfloat16),
            pltpu.VMEM((3, 8, 16, 128), F32),
            pltpu.VMEM((8, 16, 128), F32),
            pltpu.VMEM((8, 16, 128), F32),
            pltpu.VMEM((2, 8, 8, 128), F32),
            pltpu.VMEM((2, 2, 8, 8, 128), F32),
            pltpu.VMEM((2, 8, 128), F32),
            pltpu.VMEM((24, 128), F32),
            pltpu.VMEM((16, 128), F32),
            dma((12,)),
            dma((2, 2, 2)),
            dma((2, 2, 2)),
            dma((2, 2, 3)),
            dma((2, 2, 3)),
            dma((2, 2, 3)),
            dma((2, 2, 3)),
            dma((2,)),
            dma((2,)),
            pltpu.SemaphoreType.REGULAR,
        ],
        compiler_params=pltpu.CompilerParams(
            collective_id=0, has_side_effects=True, vmem_limit_bytes=40 * 1024 * 1024
        ),
        name="tangent",
    )(guess, right_side, diag_block, neighbour_blocks, dissipation, omega_volume, pseudo_step, phase)
    return field, norms[0, :2]


def solution(mesh):
    placed = (
        P(None, None, "pitch", "span", "axial"),
        P(None, None, "pitch", "span", "axial"),
        P(None, None, "pitch", "span", "axial"),
        P(None, None, None, "pitch", "span", "axial"),
        P(None, "pitch", "span", "axial"),
        P("pitch", "span", "axial"),
        P("pitch", "span", "axial"),
        P(),
    )
    return jax.shard_map(
        body,
        mesh=mesh,
        in_specs=placed,
        out_specs=(P(None, None, "pitch", "span", "axial"), P()),
        check_vma=False,
    )
```

time: 195 us -> 55.3 us (0.28)
  blocking collectives: 65.3 us -> 0 us
  other arithmetic: 54.7 us -> 0 us
  Pallas kernels: 0 us -> 42.9 us
  local copies, waits for them, and re-layouts: 37.7 us -> 10.5 us
  starting transfers between devices: 21.9 us -> 0 us
  waiting for transfers between devices: 12.8 us -> 0 us
    psum x1 -> x0, blocking collectives: 65.3 us -> none  [body(): global_sums.append(lax.psum(local_square, ('pitch', 'span', 'axial')))]
    pallas_call x0 -> x1, Pallas kernels: none -> 42.9 us  [body(): pl.pallas_call(kernel, out_shape=(jax.ShapeDtypeStruct(guess.shape, F32),...]
    reduce_sum x2 -> x0, other arithmetic: 24.4 us -> none  [body(): local_square = jnp.sum(residual * residual)]
    ppermute x12 -> x0, starting transfers between devices: 21.9 us -> none  [the longest x6 14 us: extended_2(): lax.ppermute(head, axis, [((i + 1) % count, i) for i in range(count)])]
    slice x10 -> x0, local copies, waits for them, and re-layouts: 17.8 us -> none  [the longest x7 10.9 us: extended_2(): lax.slice_in_dim(cells, cells.shape[dim] - width, cells.shape[dim], axis=...]
    ppermute x12 -> x0, waiting for transfers between devices: 12.8 us -> none  [the longest x6 9.99 us: extended_2(): lax.ppermute(tail, axis, [(i, (i + 1) % count) for i in range(count)])]
    mul x13 -> x0, other arithmetic: 12.6 us -> none  [the longest x11 10.7 us: block_apply(): blocks[:, column].astype(jnp.float32)[None] * vector_in[:, column][:, None]]
    convert_element_type x7 -> x0, other arithmetic: 10.1 us -> none  [block_apply(): blocks[:, column].astype(jnp.float32)[None] * vector_in[:, column][:, None]]
  transfers between devices with their start and end apart: 12 -> 0, of which waited for: 5 -> 0; matrix products, arithmetic and copies ran while one was open for 21% -> 0% of each run, Pallas kernels for 0% -> 0%
where the time goes in v1:
time: 55.3 us; the launch traced here: 54.7 us
  Pallas kernels  42.9 us (78%)
  local copies, waits for them, and re-layouts  10.5 us (19%)
  between operations  1.3 us (2%)
    pallas_call x1, Pallas kernels, body(): pl.pallas_call(kernel, out_shape=(jax.ShapeDtypeStruct(guess.shape, F32),...  42.9 us
    unnamed x15, local copies, waits for them, and re-layouts  10 us

profile of v1, /device:TPU:1, one launch (start us, length us, event | category | flops | bytes accessed | tf_op | source)
XLA Modules:
  0.0 54.7 jit_solution(13326672436490455835)
XLA Ops:
  1.3 0.0 copy-start
  1.3 3.0 %copy-done = bf16[6,6,6,8,16,128]{5,4,3,2,1,0:T(8,128)(2,1)S(1)} copy-done((bf16[6,6,6,8,16,128]{5,4,3,2,1,0:T(8,128)(2,1)S(1)}, bf16[6,6,6,8,16,128]{5,4,3,2,1,0:T(8,128)(2,1)}, u32[]{:S(2)}) %copy-start) | copy-done | bytes 7077912
  4.3 0.0 copy-start.1
  4.3 1.3 %copy-done.1 = bf16[6,6,8,16,128]{4,3,2,1,0:T(8,128)(2,1)S(1)} copy-done((bf16[6,6,8,16,128]{4,3,2,1,0:T(8,128)(2,1)S(1)}, bf16[6,6,8,16,128]{4,3,2,1,0:T(8,128)(2,1)}, u32[]{:S(2)}) %copy-start.1) | copy-done | bytes 1179672
  5.6 0.0 copy-start.2
  5.6 1.1 %copy-done.2 = f32[2,6,8,16,128]{4,3,2,1,0:T(8,128)S(1)} copy-done((f32[2,6,8,16,128]{4,3,2,1,0:T(8,128)S(1)}, f32[2,6,8,16,128]{4,3,2,1,0:T(8,128)}, u32[]{:S(2)}) %copy-start.2) | copy-done | bytes 786456
  6.7 0.0 copy-start.3
  6.7 1.1 %copy-done.3 = f32[2,6,8,16,128]{4,3,2,1,0:T(8,128)S(1)} copy-done((f32[2,6,8,16,128]{4,3,2,1,0:T(8,128)S(1)}, f32[2,6,8,16,128]{4,3,2,1,0:T(8,128)}, u32[]{:S(2)}) %copy-start.3) | copy-done | bytes 786456
  7.8 0.0 copy-start.4
  7.8 0.9 %copy-done.4 = f32[3,8,16,128]{3,2,1,0:T(8,128)S(1)} copy-done((f32[3,8,16,128]{3,2,1,0:T(8,128)S(1)}, f32[3,8,16,128]{3,2,1,0:T(8,128)}, u32[]{:S(2)}) %copy-start.4) | copy-done | bytes 196632
  8.8 0.0 copy-start.5
  8.8 0.8 %copy-done.5 = f32[8,16,128]{2,1,0:T(8,128)S(1)} copy-done((f32[8,16,128]{2,1,0:T(8,128)S(1)}, f32[8,16,128]{2,1,0:T(8,128)}, u32[]{:S(2)}) %copy-start.5) | copy-done | bytes 65560
  9.6 0.0 copy-start.6
  9.6 0.8 %copy-done.6 = f32[8,16,128]{2,1,0:T(8,128)S(1)} copy-done((f32[8,16,128]{2,1,0:T(8,128)S(1)}, f32[8,16,128]{2,1,0:T(8,128)}, u32[]{:S(2)}) %copy-start.6) | copy-done | bytes 65560
  10.4 42.9 %tangent.1 = (f32[2,6,8,16,128]{4,3,2,1,0:T(8,128)S(1)}, f32[1,128]{1,0:T(1,128)S(1)}) custom-call(f32[2,6,8,16,128]{4,3,2,1,0:T(8,128)S(1)} %copy-done.2, f32[2,6,8,16,128]{4,3,2,1,0:T(8,128)S(1)} %copy-done.3, bf16[6,6,8,16,128]{4,3,2,1,0:T(8,128)(2,1)S(1)} %copy-done.1, bf16[6,6,6,8,16,128]{5,4,3,2,1,0:T(8,128)(2,1)S(1)} %copy-done, ...), custom_call_target="tpu_custom_call" | custom-call | tf_op jit(solution)/shard_map/tangent/pallas_call | solution.py:386
  53.3 0.5 slice_bitcast_fusion
  53.8 0.9 %copy.12 = f32[2,6,8,16,128]{4,3,2,1,0:T(8,128)} copy(f32[2,6,8,16,128]{4,3,2,1,0:T(8,128)S(1)} %get-tuple-element.8) | data formatting | bytes 1572864
Async XLA Ops:
  1.3 3.0 %copy-start = (bf16[6,6,6,8,16,128]{5,4,3,2,1,0:T(8,128)(2,1)S(1)}, bf16[6,6,6,8,16,128]{5,4,3,2,1,0:T(8,128)(2,1)}, u32[]{:S(2)}) copy-start(bf16[6,6,6,8,16,128]{5,4,3,2,1,0:T(8,128)(2,1)} %neigh_h.1) | copy-start | bytes 21233668
  4.3 1.3 %copy-start.1 = (bf16[6,6,8,16,128]{4,3,2,1,0:T(8,128)(2,1)S(1)}, bf16[6,6,8,16,128]{4,3,2,1,0:T(8,128)(2,1)}, u32[]{:S(2)}) copy-start(bf16[6,6,8,16,128]{4,3,2,1,0:T(8,128)(2,1)} %diag_h.1) | copy-start | bytes 3538948
  5.6 1.1 %copy-start.2 = (f32[2,6,8,16,128]{4,3,2,1,0:T(8,128)S(1)}, f32[2,6,8,16,128]{4,3,2,1,0:T(8,128)}, u32[]{:S(2)}) copy-start(f32[2,6,8,16,128]{4,3,2,1,0:T(8,128)} %guess.1) | copy-start | bytes 2359300
  6.7 1.1 %copy-start.3 = (f32[2,6,8,16,128]{4,3,2,1,0:T(8,128)S(1)}, f32[2,6,8,16,128]{4,3,2,1,0:T(8,128)}, u32[]{:S(2)}) copy-start(f32[2,6,8,16,128]{4,3,2,1,0:T(8,128)} %right_h.1) | copy-start | bytes 2359300
  7.8 0.9 %copy-start.4 = (f32[3,8,16,128]{3,2,1,0:T(8,128)S(1)}, f32[3,8,16,128]{3,2,1,0:T(8,128)}, u32[]{:S(2)}) copy-start(f32[3,8,16,128]{3,2,1,0:T(8,128)} %diss_h.1) | copy-start | bytes 589828
  8.8 0.8 %copy-start.5 = (f32[8,16,128]{2,1,0:T(8,128)S(1)}, f32[8,16,128]{2,1,0:T(8,128)}, u32[]{:S(2)}) copy-start(f32[8,16,128]{2,1,0:T(8,128)} %omega_h.1) | copy-start | bytes 196612
  9.6 0.8 %copy-start.6 = (f32[8,16,128]{2,1,0:T(8,128)S(1)}, f32[8,16,128]{2,1,0:T(8,128)}, u32[]{:S(2)}) copy-start(f32[8,16,128]{2,1,0:T(8,128)} %pseudo_h.1) | copy-start | bytes 196612

commit v2 on v1

v2 whole, which is shorter than its diff:
```python
import functools

import jax
import jax.numpy as jnp
from jax import lax
from jax.experimental import pallas as pl
from jax.experimental.pallas import tpu as pltpu
from jax.sharding import PartitionSpec as P

ITERS = 2
MESH = pl.DeviceIdType.MESH
F32 = jnp.float32


def kernel(
    guess, right_h, diag_h, neigh_h, diss_h, omega_h, pseudo_h, phase_h,
    out, norms,
    st, hal, prt, rs, dg, nb, ds, om, ps, axs, axr, sq, red, tot_s, phase,
    ld_sem, psend, precv, zsend, zrecv, asend, arecv, rsend, rrecv, ready,
):
    p, s, a = lax.axis_index("pitch"), lax.axis_index("span"), lax.axis_index("axial")
    size_p, size_s, size_a = lax.axis_size("pitch"), lax.axis_size("span"), lax.axis_size("axial")
    y, x_hi = p // 2, lax.rem(p, 2)

    def row_peer(d):
        k = lax.rem(x_hi * size_a + a + d, 2 * size_a)
        return (y * 2 + k // size_a, s, lax.rem(k, size_a))

    def plane_peer(d):
        dy, dz = d // 4, d % 4
        return (lax.rem(p + 2 * dy, size_p), lax.rem(s + dz, size_s), a)

    other = lax.rem(p - 1 + 2 * x_hi + size_p, size_p)
    bar = pltpu.get_barrier_semaphore()
    peers = [(other, s, a)]
    peers += [row_peer(d) for d in range(1, 8)]
    peers += [plane_peer(4 * d) for d in range(1, 4)]
    peers += [plane_peer(d) for d in range(1, 4)]
    for peer in peers:
        pl.semaphore_signal(bar, inc=1, device_id=peer, device_id_type=MESH)

    loads = [
        pltpu.make_async_copy(guess, st.at[0, :, :, pl.ds(2, 8), pl.ds(8, 16), :], ld_sem.at[0]),
        pltpu.make_async_copy(diss_h, ds, ld_sem.at[1]),
        pltpu.make_async_copy(omega_h, om, ld_sem.at[2]),
        pltpu.make_async_copy(pseudo_h, ps, ld_sem.at[3]),
        pltpu.make_async_copy(right_h, rs, ld_sem.at[4]),
        pltpu.make_async_copy(diag_h, dg, ld_sem.at[5]),
    ] + [pltpu.make_async_copy(neigh_h.at[d], nb.at[d], ld_sem.at[6 + d]) for d in range(6)]
    phase_load = pltpu.make_async_copy(phase_h, phase, ld_sem.at[12])
    phase_load.start()
    for load in loads:
        load.start()

    rows_zero = jnp.zeros((2, 2, 6, 8, 2, 128), F32)
    ax_zero = jnp.zeros((2, 8, 8, 128), F32)
    layers_zero = jnp.zeros((2, 2, 6, 2, 16, 128), F32)
    st[:, :, :, 0:2, 8:24, :] = layers_zero
    st[:, :, :, 10:12, 8:24, :] = layers_zero

    @pl.when(s == 0)
    def _():
        st[:, :, :, 2:10, 6:8, :] = rows_zero

    @pl.when(s == size_s - 1)
    def _():
        st[:, :, :, 2:10, 24:26, :] = rows_zero

    @pl.when(a == 0)
    def _():
        axr[:, 0] = ax_zero

    @pl.when(a == size_a - 1)
    def _():
        axr[:, 1] = ax_zero

    sq[...] = jnp.zeros((2, 8, 128), F32)
    phase_load.wait()
    angle = jnp.full((8, 128), phase[0], F32)
    cosine, sine = jnp.cos(angle), jnp.sin(angle)
    first, last = p == 0, p == size_p - 1
    turn_cos = jnp.where(first | last, cosine, 1.0)
    turn_sin = jnp.where(first, -sine, jnp.where(last, sine, 0.0))
    lane = lax.broadcasted_iota(jnp.int32, (8, 128), 1)
    lane16 = lax.broadcasted_iota(jnp.int32, (16, 128), 1)
    faces = (x_hi, 1 - x_hi)
    OTHER, SAME = 0, 1

    pl.semaphore_wait(bar, len(peers))

    def pitch_copy(it, kind, t):
        face = faces[kind]
        layers = pl.ds(6 * face, 2)
        if it == 0:
            src = guess.at[:, :, layers, pl.ds(8 * t, 8), :]
        else:
            src = st.at[1, :, :, pl.ds(2 + 6 * face, 2), pl.ds(8 + 8 * t, 8), :]
        return pltpu.make_async_remote_copy(
            src_ref=src,
            dst_ref=hal.at[it, kind, :, :, :, pl.ds(8 * t, 8), :],
            send_sem=psend.at[it, kind, t],
            recv_sem=precv.at[it, kind, t],
            device_id=(lax.rem(p + size_p - 1 + 2 * face, size_p), s, a),
            device_id_type=MESH,
        )

    INNER = 2
    groups = ((6 * faces[0], 2), (6 * faces[1], 2), (2, 4))

    def span_copy(it, way, group):
        first_layer, count = (0, 8) if it == 0 else groups[group]
        row = 0 if way == 0 else 14
        if it == 0:
            src = guess.at[:, :, pl.ds(first_layer, count), pl.ds(row, 2), :]
        else:
            src = st.at[1, :, :, pl.ds(2 + first_layer, count), pl.ds(8 + row, 2), :]
        return pltpu.make_async_remote_copy(
            src_ref=src,
            dst_ref=st.at[it, :, :, pl.ds(2 + first_layer, count), pl.ds(24 if way == 0 else 6, 2), :],
            send_sem=zsend.at[it, way, group],
            recv_sem=zrecv.at[it, 1 - way, group],
            device_id=(p, lax.rem(s + (size_s - 1 if way == 0 else 1), size_s), a),
            device_id_type=MESH,
        )

    def axial_copy(it, way, group):
        first_layer, count = (0, 8) if it == 0 else groups[group]
        return pltpu.make_async_remote_copy(
            src_ref=axs.at[it, pl.ds(first_layer, count)],
            dst_ref=axr.at[it, 1 - way, pl.ds(first_layer, count)],
            send_sem=asend.at[it, way, group],
            recv_sem=arecv.at[it, 1 - way, group],
            device_id=(p, s, lax.rem(a + (size_a - 1 if way == 0 else 1), size_a)),
            device_id_type=MESH,
        )

    has_span = (s > 0, s < size_s - 1)
    has_axial = (a > 0, a < size_a - 1)

    def span_start(it, way, group):
        @pl.when(has_span[way])
        def _():
            span_copy(it, way, group).start()

    def axial_start(it, group):
        for way in range(2):
            @pl.when(has_axial[way])
            def _():
                axial_copy(it, way, group).start()

    def side_wait(it, group):
        for way in range(2):
            @pl.when(has_span[way])
            def _():
                span_copy(it, 1 - way, group).wait_recv()

            @pl.when(has_axial[way])
            def _():
                axial_copy(it, 1 - way, group).wait_recv()

    def side_drain(it, group):
        for way in range(2):
            @pl.when(has_span[way])
            def _():
                span_copy(it, way, group).wait_send()

            @pl.when(has_axial[way])
            def _():
                axial_copy(it, way, group).wait_send()

    def over(count, layer_of, work):
        def step(i, carry):
            work(layer_of(i))
            return carry

        lax.fori_loop(0, count, step, 0)

    def pack(it, q):
        packed = jnp.zeros((8, 128), F32)
        for c in range(2):
            for v in range(6):
                for t in range(2):
                    k = (c * 6 + v) * 2 + t
                    tile = st[it, c, v, q + 2, 8 + 8 * t : 16 + 8 * t, :]
                    packed = jnp.where(lane // 4 == k, pltpu.roll(tile, 4 * k + 2, 1), packed)
        axs[it, q] = packed

    def store(it, q, rows, c, v, residual, state):
        new = state + ps[q, rows, :] * residual
        if it == ITERS - 1:
            out[c, v, q, rows, :] = new
        else:
            st[1, c, v, q + 2, pl.ds(8 + rows.start, rows.size), :] = new

    def add_square(it, residuals):
        total = sq[it]
        for residual in residuals:
            square = residual * residual
            for t in range(residual.shape[0] // 8):
                total = total + square[8 * t : 8 * t + 8]
        sq[it] = total

    def times(left, block_of, values):
        for i in range(6):
            block = block_of(i).astype(F32)
            for c in range(2):
                left[c][i] = left[c][i] - block * values[c]

    def own_terms(it, q):
        left = [[rs[c, i, q] for i in range(6)] for c in range(2)]
        for j in range(6):
            times(left, lambda i: dg[i, j, q], [st[it, c, j, q + 2, 8:24, :] for c in range(2)])
        for d in range(2):
            for j in range(6):
                times(left, lambda i: nb[d, i, j, q], [st[it, c, j, q + 1 + 2 * d, 8:24, :] for c in range(2)])
        for i in range(6):
            for c in range(2):
                value = left[c][i]
                value = value - ds[0, q] * (st[it, c, i, q, 8:24, :] + st[it, c, i, q + 4, 8:24, :])
                turned = om[q] * st[it, 1 - c, i, q + 2, 8:24, :]
                prt[c, i, q] = value + turned if c == 0 else value - turned

    def side_terms(it, q, keep):
        left = [[prt[c, i, q] for i in range(6)] for c in range(2)]
        for d in range(2):
            for j in range(6):
                times(left, lambda i: nb[2 + d, i, j, q], [st[it, c, j, q + 2, 7 + 2 * d : 23 + 2 * d, :] for c in range(2)])
        mixed = jnp.where(lax.rem(lane, 4) < 2, axr[it, 0, q], axr[it, 1, q])
        for j in range(6):
            below, above = [], []
            for c in range(2):
                u = st[it, c, j, q + 2, 8:24, :]
                k = (c * 6 + j) * 2
                rim = jnp.concatenate([pltpu.roll(mixed, 126 - 4 * (k + t), 1) for t in range(2)], axis=0)
                below.append(pltpu.roll(jnp.where(lane16 == 127, rim, u), 1, 1))
                above.append(pltpu.roll(jnp.where(lane16 == 0, rim, u), 127, 1))
                left[c][j] = left[c][j] - ds[2, q] * (
                    pltpu.roll(jnp.where(lane16 >= 126, rim, u), 2, 1)
                    + pltpu.roll(jnp.where(lane16 < 2, rim, u), 126, 1)
                )
            times(left, lambda i: nb[4, i, j, q], below)
            times(left, lambda i: nb[5, i, j, q], above)
        for i in range(6):
            for c in range(2):
                left[c][i] = left[c][i] - ds[1, q] * (
                    st[it, c, i, q + 2, 6:22, :] + st[it, c, i, q + 2, 10:26, :]
                )
                if keep:
                    prt[c, i, q] = left[c][i]
                else:
                    store(it, q, pl.ds(0, 16), c, i, left[c][i], st[it, c, i, q + 2, 8:24, :])
        if not keep:
            add_square(it, left[0] + left[1])

    def finish(it, kind, t):
        rows = pl.ds(8 * t, 8)
        body_rows = pl.ds(8 + 8 * t, 8)
        face = faces[kind]

        def rim(at):
            real = [hal[it, kind, 0, j, at, rows, :] for j in range(6)]
            imag = [hal[it, kind, 1, j, at, rows, :] for j in range(6)]
            if kind == SAME:
                return [real, imag]
            return [
                [turn_cos * x - turn_sin * w for x, w in zip(real, imag)],
                [turn_sin * x + turn_cos * w for x, w in zip(real, imag)],
            ]

        near, far = rim(1 - face), rim(face)
        edge, second = 7 * face, 1 + 5 * face
        left = [[prt[c, i, edge, rows, :] for i in range(6)] for c in range(2)]
        for j in range(6):
            times(left, lambda i: nb[face, i, j, edge, rows, :], [near[c][j] for c in range(2)])
        squares = []
        for c in range(2):
            for i in range(6):
                residual = left[c][i] - ds[0, edge, rows, :] * far[c][i]
                squares.append(residual)
                store(it, edge, rows, c, i, residual, st[it, c, i, edge + 2, body_rows, :])
                residual = prt[c, i, second, rows, :] - ds[0, second, rows, :] * near[c][i]
                squares.append(residual)
                store(it, second, rows, c, i, residual, st[it, c, i, second + 2, body_rows, :])
        add_square(it, squares)

    every = (8, lambda i: i)
    inner = (4, lambda i: i + 2)
    outer = (4, lambda i: i + 4 * (i // 2))
    order = ((0, OTHER), (0, SAME), (1, OTHER), (1, SAME))

    for way in range(2):
        span_start(0, way, 0)
    for t, kind in order:
        pitch_copy(0, kind, t).start()
    for d in range(1, 4):
        pl.semaphore_signal(ready, inc=1, device_id=plane_peer(d), device_id_type=MESH)
    loads[0].wait()
    over(*every, lambda q: pack(0, q))
    axial_start(0, 0)
    for load in loads[1:]:
        load.wait()
    over(*every, lambda q: own_terms(0, q))
    side_wait(0, 0)
    over(*outer, lambda q: side_terms(0, q, True))
    over(*inner, lambda q: side_terms(0, q, False))
    for way in range(2):
        span_start(1, way, INNER)
    over(*inner, lambda q: pack(1, q))
    axial_start(1, INNER)
    for t, kind in order:
        pitch_copy(0, kind, t).wait_recv()
        finish(0, kind, t)
        pitch_copy(1, kind, t).start()
        span_start(1, t, kind)
    over(*outer, lambda q: pack(1, q))
    for kind in range(2):
        axial_start(1, kind)

    over(*every, lambda q: own_terms(1, q))
    side_wait(1, INNER)
    over(*inner, lambda q: side_terms(1, q, False))
    for kind in range(2):
        side_wait(1, kind)
    over(*outer, lambda q: side_terms(1, q, True))
    for t, kind in order:
        pitch_copy(1, kind, t).wait_recv()
        finish(1, kind, t)

    half = lax.broadcasted_iota(jnp.int32, (1, 128), 1) < 64

    def folded(it):
        row = jnp.sum(sq[it], axis=0, keepdims=True)
        return row + pltpu.roll(row, 64, 1)

    total = jnp.where(half, folded(0), folded(1))
    row_index, plane_index = x_hi * size_a + a, y * size_s + s
    for stage in range(2):
        count = (8, 16)[stage]
        base = (0, 8)[stage]
        mine = base + (row_index, plane_index)[stage]
        peer_of = (row_peer, plane_peer)[stage]
        tot_s[pl.ds(8 * stage, 1)] = total
        if stage == 1:
            pl.semaphore_wait(ready, 3)
        for d in range(1, count):
            pltpu.make_async_remote_copy(
                src_ref=tot_s.at[pl.ds(8 * stage, 1)],
                dst_ref=red.at[pl.ds(mine, 1)],
                send_sem=rsend.at[stage],
                recv_sem=rrecv.at[stage],
                device_id=peer_of(d),
                device_id_type=MESH,
            ).start()
        got = red.at[pl.ds(base, count - 1)]
        pltpu.make_async_copy(got, got, rrecv.at[stage]).wait()
        rows = red[base : base + count]
        index = lax.broadcasted_iota(jnp.int32, (count, 128), 0) + base
        total = total + jnp.sum(jnp.where(index == mine, 0.0, rows), axis=0, keepdims=True)
    first_sum = jnp.sum(jnp.where(half, total, 0.0), axis=1, keepdims=True)
    second_sum = jnp.sum(jnp.where(half, 0.0, total), axis=1, keepdims=True)
    cells = float(12 * 8 * 16 * 128) * (size_p * size_s * size_a)
    lane1 = lax.broadcasted_iota(jnp.int32, (1, 128), 1)
    norms[...] = jnp.sqrt(jnp.where(lane1 == 0, first_sum, second_sum) / cells)

    for it in range(2):
        for t in range(2):
            for kind in range(2):
                pitch_copy(it, kind, t).wait_send()
        for group in range(1 if it == 0 else 3):
            side_drain(it, group)
    for stage in range(2):
        count = (8, 16)[stage]
        sent = red.at[pl.ds((0, 8)[stage], count - 1)]
        pltpu.make_async_copy(sent, sent, rsend.at[stage]).wait()


def body(guess, right_side, diag_block, neighbour_blocks, dissipation, omega_volume, pseudo_step, phase):
    anywhere = pl.BlockSpec(memory_space=pltpu.HBM)
    dma = pltpu.SemaphoreType.DMA
    field, norms = pl.pallas_call(
        kernel,
        out_shape=(
            jax.ShapeDtypeStruct(guess.shape, F32),
            jax.ShapeDtypeStruct((1, 128), F32),
        ),
        in_specs=[anywhere] * 8,
        out_specs=(pl.BlockSpec(memory_space=pltpu.VMEM), pl.BlockSpec(memory_space=pltpu.VMEM)),
        scratch_shapes=[
            pltpu.VMEM((2, 2, 6, 12, 32, 128), F32),
            pltpu.VMEM((2, 2, 2, 6, 2, 16, 128), F32),
            pltpu.VMEM((2, 6, 8, 16, 128), F32),
            pltpu.VMEM((2, 6, 8, 16, 128), F32),
            pltpu.VMEM((6, 6, 8, 16, 128), jnp.bfloat16),
            pltpu.VMEM((6, 6, 6, 8, 16, 128), jnp.bfloat16),
            pltpu.VMEM((3, 8, 16, 128), F32),
            pltpu.VMEM((8, 16, 128), F32),
            pltpu.VMEM((8, 16, 128), F32),
            pltpu.VMEM((2, 8, 8, 128), F32),
            pltpu.VMEM((2, 2, 8, 8, 128), F32),
            pltpu.VMEM((2, 8, 128), F32),
            pltpu.VMEM((24, 128), F32),
            pltpu.VMEM((16, 128), F32),
            pltpu.SMEM((1,), F32),
            dma((14,)),
            dma((2, 2, 2)),
            dma((2, 2, 2)),
            dma((2, 2, 3)),
            dma((2, 2, 3)),
            dma((2, 2, 3)),
            dma((2, 2, 3)),
            dma((2,)),
            dma((2,)),
            pltpu.SemaphoreType.REGULAR,
        ],
        compiler_params=pltpu.CompilerParams(
            collective_id=0, has_side_effects=True, vmem_limit_bytes=40 * 1024 * 1024
        ),
        name="tangent",
    )(*(
        pltpu.with_memory_space_constraint(operand, pltpu.HBM)
        for operand in (
            guess, right_side, diag_block, neighbour_blocks, dissipation, omega_volume, pseudo_step
        )
    ), phase)
    return field, norms[0, :2]


def solution(mesh):
    placed = (
        P(None, None, "pitch", "span", "axial"),
        P(None, None, "pitch", "span", "axial"),
        P(None, None, "pitch", "span", "axial"),
        P(None, None, None, "pitch", "span", "axial"),
        P(None, "pitch", "span", "axial"),
        P("pitch", "span", "axial"),
        P("pitch", "span", "axial"),
        P(),
    )
    return jax.shard_map(
        body,
        mesh=mesh,
        in_specs=placed,
        out_specs=(P(None, None, "pitch", "span", "axial"), P()),
        check_vma=False,
    )
```

time: 55.3 us -> 42.2 us (0.76)
  local copies, waits for them, and re-layouts: 10.5 us -> 1.39 us
  Pallas kernels: 42.9 us -> 39.2 us
    unnamed x15 -> x1, local copies, waits for them, and re-layouts: 10 us -> 0.88 us
    pallas_call x1, Pallas kernels: 42.9 us -> 39.2 us  [body(): pl.pallas_call(kernel, out_shape=(jax.ShapeDtypeStruct(guess.shape, F32),...]
where the time goes in v2:
time: 42.2 us; the launch traced here: 41.9 us
  Pallas kernels  39.2 us (93%)
  local copies, waits for them, and re-layouts  1.39 us (3%)
  between operations  1.29 us (3%)
    pallas_call x1, Pallas kernels, body(): pl.pallas_call(kernel, out_shape=(jax.ShapeDtypeStruct(guess.shape, F32),...  39.2 us
    unnamed x1, local copies, waits for them, and re-layouts  0.88 us

profile of v2, /device:TPU:1, one launch (start us, length us, event | category | flops | bytes accessed | tf_op | source)
XLA Modules:
  0.0 41.9 jit_solution(11620888825267251025)
XLA Ops:
  1.3 39.2 %tangent.1 = (f32[2,6,8,16,128]{4,3,2,1,0:T(8,128)S(1)}, f32[1,128]{1,0:T(1,128)S(1)}) custom-call(f32[2,6,8,16,128]{4,3,2,1,0:T(8,128)} %guess.1, f32[2,6,8,16,128]{4,3,2,1,0:T(8,128)} %right_h.1, bf16[6,6,8,16,128]{4,3,2,1,0:T(8,128)(2,1)} %diag_h.1, bf16[6,6,6,8,16,128]{5,4,3,2,1,0:T(8,128)(2,1)} %neigh_h.1, f32[3,8,16,128]{3,2,1,0:T(8,128)} %diss_h.1, ...), custom_call_target="tpu_custom_call" | custom-call | tf_op jit(solution)/shard_map/tangent/pallas_call | solution.py:380
  40.5 0.5 %slice_bitcast_fusion = f32[2]{0:T(128)} fusion(f32[1,128]{1,0:T(1,128)S(1)} %get-tuple-element.5), kind=kLoop, calls=%fused_computation | loop fusion | bytes 16 | tf_op jit(solution)/shard_map/squeeze | solution.py:425
  41.0 0.9 %copy.12 = f32[2,6,8,16,128]{4,3,2,1,0:T(8,128)} copy(f32[2,6,8,16,128]{4,3,2,1,0:T(8,128)S(1)} %get-tuple-element.8) | data formatting | bytes 1572864

commit v3 on v2

--- a/solution.py
+++ b/solution.py
@@ -16,7 +16,7 @@
     guess, right_h, diag_h, neigh_h, diss_h, omega_h, pseudo_h, phase_h,
     out, norms,
     st, hal, prt, rs, dg, nb, ds, om, ps, axs, axr, sq, red, tot_s, phase,
-    ld_sem, psend, precv, zsend, zrecv, asend, arecv, rsend, rrecv, ready,
+    ld_sem, psend, precv, zsend, zrecv, asend, arecv, rsend, rrecv, ready, ready_row,
 ):
     p, s, a = lax.axis_index("pitch"), lax.axis_index("span"), lax.axis_index("axial")
     size_p, size_s, size_a = lax.axis_size("pitch"), lax.axis_size("span"), lax.axis_size("axial")
@@ -286,32 +286,40 @@
     every = (8, lambda i: i)
     inner = (4, lambda i: i + 2)
     outer = (4, lambda i: i + 4 * (i // 2))
-    order = ((0, OTHER), (0, SAME), (1, OTHER), (1, SAME))
-
+    kinds = (OTHER, SAME)
+    order = tuple((t, kind) for t in range(2) for kind in kinds)
+
+    pitch_copy(0, kinds[0], 0).start()
+    pitch_copy(0, kinds[1], 0).start()
     for way in range(2):
         span_start(0, way, 0)
-    for t, kind in order:
-        pitch_copy(0, kind, t).start()
-    for d in range(1, 4):
-        pl.semaphore_signal(ready, inc=1, device_id=plane_peer(d), device_id_type=MESH)
+    pitch_copy(0, kinds[0], 1).start()
+    pitch_copy(0, kinds[1], 1).start()
+    for d in range(1, 8):
+        pl.semaphore_signal(ready_row, inc=1, device_id=row_peer(d), device_id_type=MESH)
     loads[0].wait()
     over(*every, lambda q: pack(0, q))
     axial_start(0, 0)
     for load in loads[1:]:
         load.wait()
     over(*every, lambda q: own_terms(0, q))
+    pl.semaphore_wait(ready_row, 7)
+    for d in range(1, 4):
+        pl.semaphore_signal(ready, inc=1, device_id=plane_peer(d), device_id_type=MESH)
     side_wait(0, 0)
     over(*outer, lambda q: side_terms(0, q, True))
-    over(*inner, lambda q: side_terms(0, q, False))
-    for way in range(2):
-        span_start(1, way, INNER)
-    over(*inner, lambda q: pack(1, q))
-    axial_start(1, INNER)
-    for t, kind in order:
-        pitch_copy(0, kind, t).wait_recv()
-        finish(0, kind, t)
-        pitch_copy(1, kind, t).start()
-        span_start(1, t, kind)
+    for t in range(2):
+        for kind in kinds:
+            pitch_copy(0, kind, t).wait_recv()
+            finish(0, kind, t)
+            pitch_copy(1, kind, t).start()
+            span_start(1, t, kind)
+        if t == 0:
+            over(*inner, lambda q: side_terms(0, q, False))
+            for way in range(2):
+                span_start(1, way, INNER)
+            over(*inner, lambda q: pack(1, q))
+            axial_start(1, INNER)
     over(*outer, lambda q: pack(1, q))
     for kind in range(2):
         axial_start(1, kind)
@@ -333,29 +341,31 @@
         return row + pltpu.roll(row, 64, 1)
 
     total = jnp.where(half, folded(0), folded(1))
-    row_index, plane_index = x_hi * size_a + a, y * size_s + s
-    for stage in range(2):
-        count = (8, 16)[stage]
-        base = (0, 8)[stage]
-        mine = base + (row_index, plane_index)[stage]
-        peer_of = (row_peer, plane_peer)[stage]
-        tot_s[pl.ds(8 * stage, 1)] = total
-        if stage == 1:
-            pl.semaphore_wait(ready, 3)
-        for d in range(1, count):
-            pltpu.make_async_remote_copy(
-                src_ref=tot_s.at[pl.ds(8 * stage, 1)],
-                dst_ref=red.at[pl.ds(mine, 1)],
-                send_sem=rsend.at[stage],
-                recv_sem=rrecv.at[stage],
-                device_id=peer_of(d),
-                device_id_type=MESH,
-            ).start()
-        got = red.at[pl.ds(base, count - 1)]
-        pltpu.make_async_copy(got, got, rrecv.at[stage]).wait()
-        rows = red[base : base + count]
-        index = lax.broadcasted_iota(jnp.int32, (count, 128), 0) + base
-        total = total + jnp.sum(jnp.where(index == mine, 0.0, rows), axis=0, keepdims=True)
+    me = (y * size_s + s) * 8 + x_hi * size_a + a
+    tot_s[0:1] = total
+    near = (0, 1, 2, 1)
+    steps = sorted(
+        ((dy, dz, dk) for dy in range(4) for dz in range(4) for dk in range(8) if dy + dz + dk > 0),
+        key=lambda d: -(near[d[0]] + near[d[1]] + min(d[2], 8 - d[2]) / 2),
+    )
+    ys = [2 * lax.rem(y + d, size_p // 2) for d in range(4)]
+    zs = [lax.rem(s + d, size_s) for d in range(4)]
+    ks = [lax.rem(x_hi * size_a + a + d, 8) for d in range(8)]
+    ks = [(k // size_a, lax.rem(k, size_a)) for k in ks]
+    pl.semaphore_wait(ready, 3)
+    for dy, dz, dk in steps:
+        pltpu.make_async_remote_copy(
+            src_ref=tot_s.at[pl.ds(0, 1)],
+            dst_ref=red.at[pl.ds(me, 1)],
+            send_sem=rsend.at[0],
+            recv_sem=rrecv.at[0],
+            device_id=(ys[dy] + ks[dk][0], zs[dz], ks[dk][1]),
+            device_id_type=MESH,
+        ).start()
+    got = red.at[pl.ds(0, 127)]
+    pltpu.make_async_copy(got, got, rrecv.at[0]).wait()
+    index = lax.broadcasted_iota(jnp.int32, (128, 128), 0)
+    total = total + jnp.sum(jnp.where(index == me, 0.0, red[...]), axis=0, keepdims=True)
     first_sum = jnp.sum(jnp.where(half, total, 0.0), axis=1, keepdims=True)
     second_sum = jnp.sum(jnp.where(half, 0.0, total), axis=1, keepdims=True)
     cells = float(12 * 8 * 16 * 128) * (size_p * size_s * size_a)
@@ -368,10 +378,7 @@
                 pitch_copy(it, kind, t).wait_send()
         for group in range(1 if it == 0 else 3):
             side_drain(it, group)
-    for stage in range(2):
-        count = (8, 16)[stage]
-        sent = red.at[pl.ds((0, 8)[stage], count - 1)]
-        pltpu.make_async_copy(sent, sent, rsend.at[stage]).wait()
+    pltpu.make_async_copy(got, got, rsend.at[0]).wait()
 
 
 def body(guess, right_side, diag_block, neighbour_blocks, dissipation, omega_volume, pseudo_step, phase):
@@ -398,7 +405,7 @@
             pltpu.VMEM((2, 8, 8, 128), F32),
             pltpu.VMEM((2, 2, 8, 8, 128), F32),
             pltpu.VMEM((2, 8, 128), F32),
-            pltpu.VMEM((24, 128), F32),
+            pltpu.VMEM((128, 128), F32),
             pltpu.VMEM((16, 128), F32),
             pltpu.SMEM((1,), F32),
             dma((14,)),
@@ -410,6 +417,7 @@
             dma((2, 2, 3)),
             dma((2,)),
             dma((2,)),
+            pltpu.SemaphoreType.REGULAR,
             pltpu.SemaphoreType.REGULAR,
         ],
         compiler_params=pltpu.CompilerParams(

time: 42.2 us -> 39.9 us (0.945)
  Pallas kernels: 39.2 us -> 37.1 us
    pallas_call x1, Pallas kernels: 39.2 us -> 37.1 us  [body(): pl.pallas_call(kernel, out_shape=(jax.ShapeDtypeStruct(guess.shape, F32),...]
where the time goes in v3:
time: 39.9 us; the launch traced here: 39.8 us
  Pallas kernels  37.1 us (93%)
  local copies, waits for them, and re-layouts  1.39 us (3%)
  between operations  1.29 us (3%)
    pallas_call x1, Pallas kernels, body(): pl.pallas_call(kernel, out_shape=(jax.ShapeDtypeStruct(guess.shape, F32),...  37.1 us
    unnamed x1, local copies, waits for them, and re-layouts  0.88 us

profile of v3, /device:TPU:1, one launch (start us, length us, event | category | flops | bytes accessed | tf_op | source)
XLA Modules:
  0.0 39.8 jit_solution(16397526604828191035)
XLA Ops:
  1.3 37.1 %tangent.1 = (f32[2,6,8,16,128]{4,3,2,1,0:T(8,128)S(1)}, f32[1,128]{1,0:T(1,128)S(1)}) custom-call(f32[2,6,8,16,128]{4,3,2,1,0:T(8,128)} %guess.1, f32[2,6,8,16,128]{4,3,2,1,0:T(8,128)} %right_h.1, bf16[6,6,8,16,128]{4,3,2,1,0:T(8,128)(2,1)} %diag_h.1, bf16[6,6,6,8,16,128]{5,4,3,2,1,0:T(8,128)(2,1)} %neigh_h.1, f32[3,8,16,128]{3,2,1,0:T(8,128)} %diss_h.1, ...), custom_call_target="tpu_custom_call" | custom-call | tf_op jit(solution)/shard_map/tangent/pallas_call | solution.py:387
  38.4 0.5 %slice_bitcast_fusion = f32[2]{0:T(128)} fusion(f32[1,128]{1,0:T(1,128)S(1)} %get-tuple-element.5), kind=kLoop, calls=%fused_computation | loop fusion | bytes 16 | tf_op jit(solution)/shard_map/squeeze | solution.py:433
  38.9 0.9 %copy.12 = f32[2,6,8,16,128]{4,3,2,1,0:T(8,128)} copy(f32[2,6,8,16,128]{4,3,2,1,0:T(8,128)S(1)} %get-tuple-element.8) | data formatting | bytes 1572864

commit v4 on v3

--- a/solution.py
+++ b/solution.py
@@ -47,42 +47,7 @@
         pltpu.make_async_copy(right_h, rs, ld_sem.at[4]),
         pltpu.make_async_copy(diag_h, dg, ld_sem.at[5]),
     ] + [pltpu.make_async_copy(neigh_h.at[d], nb.at[d], ld_sem.at[6 + d]) for d in range(6)]
-    phase_load = pltpu.make_async_copy(phase_h, phase, ld_sem.at[12])
-    phase_load.start()
-    for load in loads:
-        load.start()
-
-    rows_zero = jnp.zeros((2, 2, 6, 8, 2, 128), F32)
-    ax_zero = jnp.zeros((2, 8, 8, 128), F32)
-    layers_zero = jnp.zeros((2, 2, 6, 2, 16, 128), F32)
-    st[:, :, :, 0:2, 8:24, :] = layers_zero
-    st[:, :, :, 10:12, 8:24, :] = layers_zero
-
-    @pl.when(s == 0)
-    def _():
-        st[:, :, :, 2:10, 6:8, :] = rows_zero
-
-    @pl.when(s == size_s - 1)
-    def _():
-        st[:, :, :, 2:10, 24:26, :] = rows_zero
-
-    @pl.when(a == 0)
-    def _():
-        axr[:, 0] = ax_zero
-
-    @pl.when(a == size_a - 1)
-    def _():
-        axr[:, 1] = ax_zero
-
-    sq[...] = jnp.zeros((2, 8, 128), F32)
-    phase_load.wait()
-    angle = jnp.full((8, 128), phase[0], F32)
-    cosine, sine = jnp.cos(angle), jnp.sin(angle)
-    first, last = p == 0, p == size_p - 1
-    turn_cos = jnp.where(first | last, cosine, 1.0)
-    turn_sin = jnp.where(first, -sine, jnp.where(last, sine, 0.0))
     lane = lax.broadcasted_iota(jnp.int32, (8, 128), 1)
-    lane16 = lax.broadcasted_iota(jnp.int32, (16, 128), 1)
     faces = (x_hi, 1 - x_hi)
     OTHER, SAME = 0, 1
 
@@ -220,35 +185,38 @@
                 turned = om[q] * st[it, 1 - c, i, q + 2, 8:24, :]
                 prt[c, i, q] = value + turned if c == 0 else value - turned
 
-    def side_terms(it, q, keep):
-        left = [[prt[c, i, q] for i in range(6)] for c in range(2)]
+    def side_terms(it, q, t, keep):
+        lo = 8 + 8 * t
+        rows = pl.ds(8 * t, 8)
+        left = [[prt[c, i, q, rows, :] for i in range(6)] for c in range(2)]
         for d in range(2):
             for j in range(6):
-                times(left, lambda i: nb[2 + d, i, j, q], [st[it, c, j, q + 2, 7 + 2 * d : 23 + 2 * d, :] for c in range(2)])
+                at = lo - 1 + 2 * d
+                times(left, lambda i: nb[2 + d, i, j, q, rows, :], [st[it, c, j, q + 2, at : at + 8, :] for c in range(2)])
         mixed = jnp.where(lax.rem(lane, 4) < 2, axr[it, 0, q], axr[it, 1, q])
         for j in range(6):
             below, above = [], []
             for c in range(2):
-                u = st[it, c, j, q + 2, 8:24, :]
-                k = (c * 6 + j) * 2
-                rim = jnp.concatenate([pltpu.roll(mixed, 126 - 4 * (k + t), 1) for t in range(2)], axis=0)
-                below.append(pltpu.roll(jnp.where(lane16 == 127, rim, u), 1, 1))
-                above.append(pltpu.roll(jnp.where(lane16 == 0, rim, u), 127, 1))
-                left[c][j] = left[c][j] - ds[2, q] * (
-                    pltpu.roll(jnp.where(lane16 >= 126, rim, u), 2, 1)
-                    + pltpu.roll(jnp.where(lane16 < 2, rim, u), 126, 1)
+                u = st[it, c, j, q + 2, lo : lo + 8, :]
+                k = (c * 6 + j) * 2 + t
+                rim = pltpu.roll(mixed, 126 - 4 * k, 1)
+                below.append(pltpu.roll(jnp.where(lane == 127, rim, u), 1, 1))
+                above.append(pltpu.roll(jnp.where(lane == 0, rim, u), 127, 1))
+                left[c][j] = left[c][j] - ds[2, q, rows, :] * (
+                    pltpu.roll(jnp.where(lane >= 126, rim, u), 2, 1)
+                    + pltpu.roll(jnp.where(lane < 2, rim, u), 126, 1)
                 )
-            times(left, lambda i: nb[4, i, j, q], below)
-            times(left, lambda i: nb[5, i, j, q], above)
+            times(left, lambda i: nb[4, i, j, q, rows, :], below)
+            times(left, lambda i: nb[5, i, j, q, rows, :], above)
         for i in range(6):
             for c in range(2):
-                left[c][i] = left[c][i] - ds[1, q] * (
-                    st[it, c, i, q + 2, 6:22, :] + st[it, c, i, q + 2, 10:26, :]
+                left[c][i] = left[c][i] - ds[1, q, rows, :] * (
+                    st[it, c, i, q + 2, lo - 2 : lo + 6, :] + st[it, c, i, q + 2, lo + 2 : lo + 10, :]
                 )
                 if keep:
-                    prt[c, i, q] = left[c][i]
+                    prt[c, i, q, rows, :] = left[c][i]
                 else:
-                    store(it, q, pl.ds(0, 16), c, i, left[c][i], st[it, c, i, q + 2, 8:24, :])
+                    store(it, q, rows, c, i, left[c][i], st[it, c, i, q + 2, lo : lo + 8, :])
         if not keep:
             add_square(it, left[0] + left[1])
 
@@ -295,8 +263,36 @@
         span_start(0, way, 0)
     pitch_copy(0, kinds[0], 1).start()
     pitch_copy(0, kinds[1], 1).start()
+    phase_load = pltpu.make_async_copy(phase_h, phase, ld_sem.at[12])
+    phase_load.start()
+    for load in loads:
+        load.start()
+
     for d in range(1, 8):
         pl.semaphore_signal(ready_row, inc=1, device_id=row_peer(d), device_id_type=MESH)
+    rows_zero = jnp.zeros((2, 2, 6, 8, 2, 128), F32)
+    ax_zero = jnp.zeros((2, 8, 8, 128), F32)
+    layers_zero = jnp.zeros((2, 2, 6, 2, 16, 128), F32)
+    st[:, :, :, 0:2, 8:24, :] = layers_zero
+    st[:, :, :, 10:12, 8:24, :] = layers_zero
+
+    @pl.when(s == 0)
+    def _():
+        st[:, :, :, 2:10, 6:8, :] = rows_zero
+
+    @pl.when(s == size_s - 1)
+    def _():
+        st[:, :, :, 2:10, 24:26, :] = rows_zero
+
+    @pl.when(a == 0)
+    def _():
+        axr[:, 0] = ax_zero
+
+    @pl.when(a == size_a - 1)
+    def _():
+        axr[:, 1] = ax_zero
+
+    sq[...] = jnp.zeros((2, 8, 128), F32)
     loads[0].wait()
     over(*every, lambda q: pack(0, q))
     axial_start(0, 0)
@@ -306,30 +302,39 @@
     pl.semaphore_wait(ready_row, 7)
     for d in range(1, 4):
         pl.semaphore_signal(ready, inc=1, device_id=plane_peer(d), device_id_type=MESH)
+    phase_load.wait()
+    angle = jnp.full((8, 128), phase[0], F32)
+    cosine, sine = jnp.cos(angle), jnp.sin(angle)
+    first, last = p == 0, p == size_p - 1
+    turn_cos = jnp.where(first | last, cosine, 1.0)
+    turn_sin = jnp.where(first, -sine, jnp.where(last, sine, 0.0))
     side_wait(0, 0)
-    over(*outer, lambda q: side_terms(0, q, True))
     for t in range(2):
+        over(*outer, lambda q: side_terms(0, q, t, True))
         for kind in kinds:
             pitch_copy(0, kind, t).wait_recv()
             finish(0, kind, t)
+            span_start(1, t, kind)
+            if t == 1:
+                over(2, lambda i: i + 6 * faces[kind], lambda q: pack(1, q))
+                axial_start(1, kind)
             pitch_copy(1, kind, t).start()
-            span_start(1, t, kind)
         if t == 0:
-            over(*inner, lambda q: side_terms(0, q, False))
+            for half_rows in range(2):
+                over(*inner, lambda q: side_terms(0, q, half_rows, False))
             for way in range(2):
                 span_start(1, way, INNER)
             over(*inner, lambda q: pack(1, q))
             axial_start(1, INNER)
-    over(*outer, lambda q: pack(1, q))
-    for kind in range(2):
-        axial_start(1, kind)
 
     over(*every, lambda q: own_terms(1, q))
     side_wait(1, INNER)
-    over(*inner, lambda q: side_terms(1, q, False))
+    for t in range(2):
+        over(*inner, lambda q: side_terms(1, q, t, False))
     for kind in range(2):
         side_wait(1, kind)
-    over(*outer, lambda q: side_terms(1, q, True))
+    for t in range(2):
+        over(*outer, lambda q: side_terms(1, q, t, True))
     for t, kind in order:
         pitch_copy(1, kind, t).wait_recv()
         finish(1, kind, t)

time: 39.9 us -> 39.6 us (level)
  no operation moved by 1% of the time
where the time goes in v4:
time: 39.6 us; the launch traced here: 39.5 us
  Pallas kernels  36.8 us (93%)
  local copies, waits for them, and re-layouts  1.39 us (4%)
  between operations  1.29 us (3%)
    pallas_call x1, Pallas kernels, body(): pl.pallas_call(kernel, out_shape=(jax.ShapeDtypeStruct(guess.shape, F32),...  36.8 us
    unnamed x1, local copies, waits for them, and re-layouts  0.88 us

profile of v4, /device:TPU:1, one launch (start us, length us, event | category | flops | bytes accessed | tf_op | source)
XLA Modules:
  0.0 39.5 jit_solution(10415193112105332944)
XLA Ops:
  1.3 36.8 %tangent.1 = (f32[2,6,8,16,128]{4,3,2,1,0:T(8,128)S(1)}, f32[1,128]{1,0:T(1,128)S(1)}) custom-call(f32[2,6,8,16,128]{4,3,2,1,0:T(8,128)} %guess.1, f32[2,6,8,16,128]{4,3,2,1,0:T(8,128)} %right_h.1, bf16[6,6,8,16,128]{4,3,2,1,0:T(8,128)(2,1)} %diag_h.1, bf16[6,6,6,8,16,128]{5,4,3,2,1,0:T(8,128)(2,1)} %neigh_h.1, f32[3,8,16,128]{3,2,1,0:T(8,128)} %diss_h.1, ...), custom_call_target="tpu_custom_call" | custom-call | tf_op jit(solution)/shard_map/tangent/pallas_call | solution.py:392
  38.1 0.5 %slice_bitcast_fusion = f32[2]{0:T(128)} fusion(f32[1,128]{1,0:T(1,128)S(1)} %get-tuple-element.5), kind=kLoop, calls=%fused_computation | loop fusion | bytes 16 | tf_op jit(solution)/shard_map/squeeze | solution.py:438
  38.6 0.9 %copy.12 = f32[2,6,8,16,128]{4,3,2,1,0:T(8,128)} copy(f32[2,6,8,16,128]{4,3,2,1,0:T(8,128)S(1)} %get-tuple-element.8) | data formatting | bytes 1572864

commit v5 on v4

--- a/solution.py
+++ b/solution.py
@@ -140,11 +140,11 @@
 
         lax.fori_loop(0, count, step, 0)
 
-    def pack(it, q):
-        packed = jnp.zeros((8, 128), F32)
+    def pack(it, q, halves=(0, 1)):
+        packed = jnp.zeros((8, 128), F32) if halves[0] == 0 else axs[it, q]
         for c in range(2):
             for v in range(6):
-                for t in range(2):
+                for t in halves:
                     k = (c * 6 + v) * 2 + t
                     tile = st[it, c, v, q + 2, 8 + 8 * t : 16 + 8 * t, :]
                     packed = jnp.where(lane // 4 == k, pltpu.roll(tile, 4 * k + 2, 1), packed)
@@ -316,10 +316,11 @@
             finish(0, kind, t)
             span_start(1, t, kind)
             if t == 1:
-                over(2, lambda i: i + 6 * faces[kind], lambda q: pack(1, q))
+                over(2, lambda i: i + 6 * faces[kind], lambda q: pack(1, q, (1,)))
                 axial_start(1, kind)
             pitch_copy(1, kind, t).start()
         if t == 0:
+            over(*outer, lambda q: pack(1, q, (0,)))
             for half_rows in range(2):
                 over(*inner, lambda q: side_terms(0, q, half_rows, False))
             for way in range(2):
@@ -367,6 +368,12 @@
             device_id=(ys[dy] + ks[dk][0], zs[dz], ks[dk][1]),
             device_id_type=MESH,
         ).start()
+    for it in range(2):
+        for t in range(2):
+            for kind in range(2):
+                pitch_copy(it, kind, t).wait_send()
+        for group in range(1 if it == 0 else 3):
+            side_drain(it, group)
     got = red.at[pl.ds(0, 127)]
     pltpu.make_async_copy(got, got, rrecv.at[0]).wait()
     index = lax.broadcasted_iota(jnp.int32, (128, 128), 0)
@@ -377,12 +384,6 @@
     lane1 = lax.broadcasted_iota(jnp.int32, (1, 128), 1)
     norms[...] = jnp.sqrt(jnp.where(lane1 == 0, first_sum, second_sum) / cells)
 
-    for it in range(2):
-        for t in range(2):
-            for kind in range(2):
-                pitch_copy(it, kind, t).wait_send()
-        for group in range(1 if it == 0 else 3):
-            side_drain(it, group)
     pltpu.make_async_copy(got, got, rsend.at[0]).wait()
 
 

time: 39.6 us -> 39.7 us (level)
  no operation moved by 1% of the time
where the time goes in v5:
time: 39.7 us; the launch traced here: 39.6 us
  Pallas kernels  36.9 us (93%)
  local copies, waits for them, and re-layouts  1.39 us (4%)
  between operations  1.29 us (3%)
    pallas_call x1, Pallas kernels, body(): pl.pallas_call(kernel, out_shape=(jax.ShapeDtypeStruct(guess.shape, F32),...  36.9 us
    unnamed x1, local copies, waits for them, and re-layouts  0.88 us

profile of v5, /device:TPU:1, one launch (start us, length us, event | category | flops | bytes accessed | tf_op | source)
XLA Modules:
  0.0 39.6 jit_solution(7687262034386761548)
XLA Ops:
  1.3 36.9 %tangent.1 = (f32[2,6,8,16,128]{4,3,2,1,0:T(8,128)S(1)}, f32[1,128]{1,0:T(1,128)S(1)}) custom-call(f32[2,6,8,16,128]{4,3,2,1,0:T(8,128)} %guess.1, f32[2,6,8,16,128]{4,3,2,1,0:T(8,128)} %right_h.1, bf16[6,6,8,16,128]{4,3,2,1,0:T(8,128)(2,1)} %diag_h.1, bf16[6,6,6,8,16,128]{5,4,3,2,1,0:T(8,128)(2,1)} %neigh_h.1, f32[3,8,16,128]{3,2,1,0:T(8,128)} %diss_h.1, ...), custom_call_target="tpu_custom_call" | custom-call | tf_op jit(solution)/shard_map/tangent/pallas_call | solution.py:393
  38.2 0.5 %slice_bitcast_fusion = f32[2]{0:T(128)} fusion(f32[1,128]{1,0:T(1,128)S(1)} %get-tuple-element.5), kind=kLoop, calls=%fused_computation | loop fusion | bytes 16 | tf_op jit(solution)/shard_map/squeeze | solution.py:439
  38.7 0.9 %copy.12 = f32[2,6,8,16,128]{4,3,2,1,0:T(8,128)} copy(f32[2,6,8,16,128]{4,3,2,1,0:T(8,128)S(1)} %get-tuple-element.8) | data formatting | bytes 1572864
